TPU v7x, 32 devices: a whole 2x2x4 slice. The times are simulated.
32 devices in a mesh: sens: 4 (over y, x), par: 8 (over z, core).
Axes of the slice: x: 2, y: 2, z: 4, core: 2. Of those that a mesh axis runs over, the one named last changes fastest.
Arguments:
- kernel: bfloat16 [2, 129, 64, 8192], P(None, None, 'sens', 'par'), may hold values from -0.0625 to 0.0625
- param: float32 [128, 2, 8192], P(None, None, 'par'), may hold values from -6 to 6
- observed: float32 [64, 128], P('sens'), may hold values from -6 to 6
- noise_scale: float32 [64], P('sens'), may hold values from 0.3 to 3
- robust_flags: int32 [64, 128], P('sens'), may hold values 0 or 1
- kappa_field: float32 [8192], P('par'), may hold values from 0.01 to 0.1
- coupling: float32 [8192], P('par'), may hold values from 0.05 to 0.2
- neighbours: int32 [8, 4], replicated, may hold values from -1 to 7, as said below
Outputs:
- gradient: float32 [128, 2, 8192], P(None, None, 'par')
- direction: float32 [128, 2, 8192], P(None, None, 'par')
Inputs may be any that keep to these rules, and one draw needn't show every extreme that they name: `neighbours`: row k lists the tiles west, east, south and north of tile k, or -1 where there is none; the tiles fill a grid of 2 columns and 4 rows in an order drawn from the seed, and the relations are mutual.
All inputs are finite; a program needn't handle non-finite values. No bound on the sum of `robust_flags` on one device may be relied on, other than what follows from the above.
Results may differ from a plain program's by a relative error of at most 0.003.
Values may be sent and summed in bfloat16 or wider, within the bound.
A program may use at most 128 MiB of HBM per device.

v0:
```python
import jax
import jax.numpy as jnp
from jax import lax
from jax.sharding import PartitionSpec as P

SWEEPS = 8
TSIDE = 32


huber_limit = 1.345


def tables(length):
    period = 2 * length
    frequency = jnp.arange(length + 1, dtype=jnp.int32)
    moment = jnp.arange(length, dtype=jnp.int32)
    phases = frequency[:, None] * moment[None, :] % period
    angles = phases.astype(jnp.float32) * (2.0 * jnp.pi / period)
    cosine = jnp.cos(angles)
    sines = jnp.sin(angles)
    forward = jnp.concatenate([cosine, -sines], 0)
    weight = (
        jnp.where((frequency == 0) | (frequency == length), 1.0, 2.0).astype(jnp.float32) / period
    )
    backward = jnp.concatenate([weight[:, None] * cosine, -weight[:, None] * sines], 0)
    return (forward, backward)


def residual_spectrum(predicted, observed, noise_scale, robust_flags, backward):
    length = observed.shape[1]
    sensor_count = predicted.shape[1]
    samples = predicted.shape[2]
    series = jnp.dot(
        backward.T, predicted.reshape(-1, sensor_count * samples), precision=lax.Precision.HIGHEST
    )
    series = series.reshape(length, sensor_count, samples)
    scaled = (series - observed.T[:, :, None]) / noise_scale[None, :, None]
    robust = jnp.where(
        robust_flags.T[:, :, None] == 1, jnp.clip(scaled, -huber_limit, huber_limit), scaled
    )
    weighted = robust / noise_scale[None, :, None]
    spectral = jnp.dot(backward, weighted.reshape(length, -1), precision=lax.Precision.HIGHEST)
    return spectral.reshape(-1, sensor_count, samples)


def neighbour_sum(values, own_row):
    row_count, cell_count = values.shape
    square = values.reshape(row_count, TSIDE, TSIDE)
    outgoing = jnp.stack([square[:, :, 0], square[:, :, -1], square[:, 0, :], square[:, -1, :]], 0)
    outgoing = outgoing.reshape(4, row_count * TSIDE)
    all_rims = lax.all_gather(outgoing.astype(jnp.bfloat16), "par", axis=0, tiled=True).astype(
        outgoing.dtype
    )

    def facing(tile, edge_index):
        picked = all_rims[jnp.maximum(tile, 0) * 4 + edge_index]
        return jnp.where(tile >= 0, picked, 0.0).reshape(row_count, TSIDE)

    west_rim = facing(own_row[0], 1)
    east_rim = facing(own_row[1], 0)
    south_rim = facing(own_row[2], 3)
    north_rim = facing(own_row[3], 2)
    column = jnp.arange(cell_count) % TSIDE
    zeros_column = jnp.zeros((row_count, 1), values.dtype)
    east_side = jnp.where(
        column == TSIDE - 1,
        jnp.repeat(east_rim, TSIDE, axis=1),
        jnp.concatenate([values[:, 1:], zeros_column], 1),
    )
    west_side = jnp.where(
        column == 0,
        jnp.repeat(west_rim, TSIDE, axis=1),
        jnp.concatenate([zeros_column, values[:, :-1]], 1),
    )
    north_side = jnp.concatenate([values[:, TSIDE:], north_rim], 1)
    south_side = jnp.concatenate([south_rim, values[:, :-TSIDE]], 1)
    return east_side + west_side + north_side + south_side


def per_device(
    kernel, param, observed, noise_scale, robust_flags, kappa_field, coupling, neighbours
):
    length, samples, cell_count = param.shape
    sensor_count = observed.shape[0]
    spectra_rows = 2 * (length + 1)
    forward, backward = tables(length)
    spectrum = jnp.dot(forward, param.reshape(length, -1), precision=lax.Precision.HIGHEST)
    spectrum = spectrum.reshape(2, length + 1, samples, cell_count).astype(jnp.bfloat16)
    product = jnp.einsum("ifsc,jfbc->ijfsb", kernel, spectrum, preferred_element_type=jnp.float32)
    partial_sum = jnp.concatenate([product[0, 0] - product[1, 1], product[0, 1] + product[1, 0]], 0)
    predicted = lax.psum(partial_sum, "par")
    adjoint = residual_spectrum(predicted, observed, noise_scale, robust_flags, backward).astype(
        jnp.bfloat16
    )
    adjoint = adjoint.reshape(2, length + 1, sensor_count, samples)
    back_product = jnp.einsum(
        "ifsc,jfsb->ijfbc", kernel, adjoint, preferred_element_type=jnp.float32
    )
    partial_grad = jnp.concatenate(
        [back_product[0, 0] + back_product[1, 1], back_product[0, 1] - back_product[1, 0]], 0
    )
    partial_grad = partial_grad.reshape(spectra_rows, samples * cell_count)
    row_block = length // lax.axis_size("sens")
    transposed = forward.T
    misfit = lax.psum_scatter(
        jnp.dot(transposed, partial_grad, precision=lax.Precision.HIGHEST),
        "sens",
        scatter_dimension=0,
        tiled=True,
    )
    field_rows = lax.dynamic_slice_in_dim(param, lax.axis_index("sens") * row_block, row_block, 0)
    block_length = field_rows.shape[0]
    flat_field = field_rows.reshape(-1, cell_count)
    misfit = misfit.reshape(-1, cell_count)
    diagonal = kappa_field + 4.0 * coupling
    own_row = neighbours[lax.axis_index("par")]
    gradient = misfit + diagonal * flat_field - coupling * neighbour_sum(flat_field, own_row)
    direction = gradient / diagonal
    for sweep in range(SWEEPS - 1):
        direction = (gradient + coupling * neighbour_sum(direction, own_row)) / diagonal
    gradient = gradient.reshape(block_length, samples, cell_count)
    direction = direction.reshape(block_length, samples, cell_count)
    return (
        lax.all_gather(gradient, "sens", axis=0, tiled=True),
        lax.all_gather(direction, "sens", axis=0, tiled=True),
    )


def solution(mesh):
    return jax.shard_map(
        per_device,
        mesh=mesh,
        in_specs=(
            P(None, None, "sens", "par"),
            P(None, None, "par"),
            P("sens", None),
            P("sens"),
            P("sens", None),
            P("par"),
            P("par"),
            P(),
        ),
        out_specs=(P(None, None, "par"), P(None, None, "par")),
        check_vma=False,
    )
```

profile of v0, /device:TPU:0, one launch (start us, length us, event | category | flops | bytes accessed | tf_op | source)
XLA Modules:
  0.0 279.7 jit_solution(1671266593527884040)
XLA Ops:
  7.2 0.3 fusion.61
  7.6 1.6 copy.337
  9.1 0.3 copy.244
  9.5 1.9 fusion.11
  11.4 13.9 %fusion.12 = f32[2,2,129,16,2]{3,4,0,1,2:T(2,128)S(1)} fusion(bf16[2,129,2,1024,1]{3,1,2,0,4:T(8,128)(2,1)S(1)} %fusion.11, bf16[2,129,16,1024]{3,2,1,0:T(8,128)(2,1)} %param.8), kind=kOutput, calls=%fused_computation.11 | convolution fusion | flops 33816576 | bytes 9576960 | tf_op jit(solution)/shard_map/ifsc,jfbc->ijfsb/dot_general | solution.py:89
  25.9 30.7 %psum.7 = f32[16,2,258]{2,0,1:T(8,128)S(1)} all-reduce(f32[16,2,258]{2,0,1:T(8,128)S(1)} %copy.250), channel_id=1, replica_groups=mesh['sens'=4,'par'=8] {'par'}, use_global_device_ids=true, to_apply=%region_0.1 | all-reduce | flops 8256 | bytes 66048 | tf_op jit(solution)/shard_map/psum | solution.py:91
  56.7 0.3 broadcast_multiply_fusion
  56.9 0.3 broadcast_multiply_fusion.1
  57.3 0.2 fusion.63
  57.5 0.3 convolution_convert_fusion.1
  57.9 0.2 copy.325
  58.1 5.4 %fusion.4 = f32[2,2,129,2,1024]{4,3,0,1,2:T(2,128)S(1)} fusion(bf16[2,129,16,2,1]{2,3,4,0,1:T(2,128)(2,1)S(1)} %copy.325, bf16[2,129,16,1024]{3,2,1,0:T(8,128)(2,1)} %param.8), kind=kOutput, calls=%fused_computation.4 | convolution fusion | flops 33816576 | bytes 12697728 | tf_op jit(solution)/shard_map/ifsc,jfsb->ijfbc/dot_general | solution.py:96
  63.5 1.1 fusion.17
  64.6 0.4 pad.88
  65.0 0.4 copy.338
  65.4 0.4 pad.89
  65.7 0.4 copy.339
  66.1 3.0 %fusion.7 = f32[128,2048]{1,0:T(8,128)} fusion(f32[258,128]{1,0:T(8,128)S(1)} %pad_maximum_fusion.1, f32[129,2048]{1,0:T(8,128)S(1)} %bitcast.187, f32[129,2048]{1,0:T(8,128)S(1)} %bitcast.186), kind=kOutput, calls=%fused_computation.5 | convolution fusion | flops 812126208 | bytes 3294208 | tf_op jit(solution)/shard_map/dot_general | solution.py:106
  69.3 0.6 fusion.152
  75.3 1.1 fusion.121
  76.4 0.3 reshape.473
  76.7 0.8 slice_reduce_fusion.1
  77.6 0.2 slice_reduce_fusion.3
  78.1 14.0 %all-gather = bf16[8,4,2048]{2,1,0:T(4,128)(2,1)S(1)} all-gather(bf16[1,4,2048]{2,1,0:T(4,128)(2,1)S(1)} %maximum_bitcast_fusion.7), channel_id=1, replica_groups=mesh['sens'=4,'par'=8] {'par'}, dimensions={0}, use_global_device_ids=true | all-gather | bytes 147456 | tf_op jit(solution)/shard_map/all_gather | solution.py:51
  92.4 0.2 copy.256
  92.8 0.2 copy.258
  93.1 0.2 reshape.447
  93.6 1.9 reduce-scatter.2.cloned.1.call-done
  95.5 1.0 reshape.446
  96.5 0.3 fusion.119
  98.2 14.3 %all-gather.1 = bf16[8,4,2048]{2,1,0:T(4,128)(2,1)S(1)} all-gather(bf16[1,4,2048]{2,1,0:T(4,128)(2,1)S(1)} %maximum_bitcast_fusion.8), channel_id=1, replica_groups=mesh['sens'=4,'par'=8] {'par'}, dimensions={0}, use_global_device_ids=true | all-gather | bytes 147456 | tf_op jit(solution)/shard_map/all_gather | solution.py:51
  112.8 0.2 copy.265
  113.1 0.2 copy.267
  113.5 0.2 fusion.117
  115.1 14.0 %all-gather.2 = bf16[8,4,2048]{2,1,0:T(4,128)(2,1)S(1)} all-gather(bf16[1,4,2048]{2,1,0:T(4,128)(2,1)S(1)} %maximum_bitcast_fusion.9), channel_id=1, replica_groups=mesh['sens'=4,'par'=8] {'par'}, dimensions={0}, use_global_device_ids=true | all-gather | bytes 147456 | tf_op jit(solution)/shard_map/all_gather | solution.py:51
  129.4 0.2 copy.274
  129.8 0.2 copy.276
  130.2 0.2 fusion.115
  131.8 14.0 %all-gather.3 = bf16[8,4,2048]{2,1,0:T(4,128)(2,1)S(1)} all-gather(bf16[1,4,2048]{2,1,0:T(4,128)(2,1)S(1)} %maximum_bitcast_fusion.10), channel_id=1, replica_groups=mesh['sens'=4,'par'=8] {'par'}, dimensions={0}, use_global_device_ids=true | all-gather | bytes 147456 | tf_op jit(solution)/shard_map/all_gather | solution.py:51
  146.1 0.2 copy.283
  146.4 0.2 copy.285
  146.8 0.2 fusion.113
  148.4 14.0 %all-gather.4 = bf16[8,4,2048]{2,1,0:T(4,128)(2,1)S(1)} all-gather(bf16[1,4,2048]{2,1,0:T(4,128)(2,1)S(1)} %maximum_bitcast_fusion.11), channel_id=1, replica_groups=mesh['sens'=4,'par'=8] {'par'}, dimensions={0}, use_global_device_ids=true | all-gather | bytes 147456 | tf_op jit(solution)/shard_map/all_gather | solution.py:51
  162.7 0.2 copy.292
  163.1 0.2 copy.294
  163.4 0.2 fusion.111
  165.0 14.0 %all-gather.5 = bf16[8,4,2048]{2,1,0:T(4,128)(2,1)S(1)} all-gather(bf16[1,4,2048]{2,1,0:T(4,128)(2,1)S(1)} %maximum_bitcast_fusion.12), channel_id=1, replica_groups=mesh['sens'=4,'par'=8] {'par'}, dimensions={0}, use_global_device_ids=true | all-gather | bytes 147456 | tf_op jit(solution)/shard_map/all_gather | solution.py:51
  179.3 0.2 copy.301
  179.7 0.2 copy.303
  180.0 0.2 fusion.109
  181.6 14.0 %all-gather.6 = bf16[8,4,2048]{2,1,0:T(4,128)(2,1)S(1)} all-gather(bf16[1,4,2048]{2,1,0:T(4,128)(2,1)S(1)} %maximum_bitcast_fusion.13), channel_id=1, replica_groups=mesh['sens'=4,'par'=8] {'par'}, dimensions={0}, use_global_device_ids=true | all-gather | bytes 147456 | tf_op jit(solution)/shard_map/all_gather | solution.py:51
  195.9 0.2 copy.310
  196.3 0.2 copy.312
  196.7 0.2 fusion.107
  198.3 14.0 %all-gather.7 = bf16[8,4,2048]{2,1,0:T(4,128)(2,1)S(1)} all-gather(bf16[1,4,2048]{2,1,0:T(4,128)(2,1)S(1)} %maximum_bitcast_fusion.14), channel_id=1, replica_groups=mesh['sens'=4,'par'=8] {'par'}, dimensions={0}, use_global_device_ids=true | all-gather | bytes 147456 | tf_op jit(solution)/shard_map/all_gather | solution.py:51
  212.6 0.2 copy.319
  213.0 0.2 copy.321
  213.3 0.3 fusion.49
  213.5 0.8 reshape.472
  214.5 0.8 reshape.450
  215.3 25.6 %all-gather.13.cloned.1.call-done = f32[128,2,1024]{2,1,0:T(2,128)} async-done(((f32[32,2,1024]{2,1,0:T(2,128)}), f32[128,2,1024]{2,1,0:T(2,128)}) %all-gather.13.cloned.1.call-update) | async-done | bytes 1048592 | tf_op jit(solution)/shard_map/all_gather | solution.py:125
  240.9 28.9 %all-gather.11.cloned.1.call-done = f32[128,2,1024]{2,1,0:T(2,128)} async-done(((f32[32,2,1024]{2,1,0:T(2,128)}), f32[128,2,1024]{2,1,0:T(2,128)}) %all-gather.11.cloned.1.call-update) | async-done | bytes 1048592 | tf_op jit(solution)/shard_map/all_gather | solution.py:124
  269.9 2.3 copy.356
  272.2 1.0 copy.357
  (221 shorter events, 15.7 us)
Async XLA Ops:
  7.2 62.1 %copy-start = (s32[8,4]{0,1:T(4,128)S(1)}, s32[8,4]{0,1:T(4,128)}, u32[]{:S(2)}) copy-start(s32[8,4]{0,1:T(4,128)} %param.15) | copy-start | bytes 388
  7.2 88.3 %reduce-scatter.2.cloned.1.call-start = ((), (), s32[]{:S(2)}) async-start(), calls=%async_computation.1 | async-start | bytes 1310720 | tf_op jit(solution)/shard_map/reduce_scatter | solution.py:105
  25.3 31.9 %copy-start.3 = (s32[16,128]{1,0:T(8,128)S(1)}, s32[16,128]{1,0:T(8,128)}, u32[]{:S(2)}) copy-start(s32[16,128]{1,0:T(8,128)} %param.12) | copy-start | bytes 24580
  25.3 31.9 %copy-start.5 = (f32[16,128]{1,0:T(8,128)S(1)}, f32[16,128]{1,0:T(8,128)}, u32[]{:S(2)}) copy-start(f32[16,128]{1,0:T(8,128)} %param.10) | copy-start | bytes 24580
  25.3 31.9 %copy-start.6 = (f32[16]{0:T(128)S(1)}, f32[16]{0:T(128)}, u32[]{:S(2)}) copy-start(f32[16]{0:T(128)} %param.11) | copy-start | bytes 196
  69.2 171.7 %all-gather.13.cloned.1.call-start = ((), (), s32[]{:S(2)}) async-start(), calls=%async_computation.3 | async-start | bytes 1310720 | tf_op jit(solution)/shard_map/all_gather | solution.py:125
  92.6 0.8 copy-start.2
  92.6 0.8 copy-start.4
  214.4 55.5 %all-gather.11.cloned.1.call-start = ((), (), s32[]{:S(2)}) async-start(), calls=%async_computation.2 | async-start | bytes 1310720 | tf_op jit(solution)/shard_map/all_gather | solution.py:124
  240.9 31.2 %copy-start.1 = (f32[128,2,1024]{2,1,0:T(2,128)S(1)}, f32[128,2,1024]{2,1,0:T(2,128)}, u32[]{:S(2)}) copy-start(f32[128,2,1024]{2,1,0:T(2,128)} %all-gather.13.cloned.1.call-done) | copy-start | bytes 3145732
Sparse Core Ops, SparseCore 0:
  69.3 26.1 reduce-scatter.1
  214.5 26.3 all-gather.12
  243.4 26.4 all-gather.10
where the time goes:
time: 280 us
  blocking collectives  143 us (51%)
  waiting for transfers between devices  56.5 us (20%)
  local copies, waits for them, and re-layouts  28.3 us (10%)
  matrix products  24.8 us (9%)
  between operations  20.3 us (7%)
  other arithmetic  6.71 us (2%)
    all_gather x8, blocking collectives, neighbour_sum(): lax.all_gather(outgoing.astype(jnp.bfloat16), 'par', axis=0, tiled=True)  112 us
    psum x1, blocking collectives, per_device(): predicted = lax.psum(partial_sum, 'par')  30.7 us
    all_gather x1, waiting for transfers between devices, per_device(): lax.all_gather(gradient, 'sens', axis=0, tiled=True)  28.9 us
    all_gather x1, waiting for transfers between devices, per_device(): lax.all_gather(direction, 'sens', axis=0, tiled=True)  25.6 us
    dot_general x1, matrix products, per_device(): jnp.einsum('ifsc,jfbc->ijfsb', kernel, spectrum, preferred_element_type=j...  13.9 us
    unnamed x21, local copies, waits for them, and re-layouts  6.34 us
  transfers between devices with their start and end apart: 3, of which 3 were waited for; matrix products, arithmetic and copies ran while one was open for 2% of the time, Pallas kernels for 0%

commit v1 on v0

v1 whole, which is shorter than its diff:
```python
import functools

import jax
import jax.numpy as jnp
from jax import lax
from jax.experimental import pallas as pl
from jax.experimental.pallas import tpu as pltpu
from jax.sharding import PartitionSpec as P

SWEEPS = 8
TSIDE = 32
LANES = 128


huber_limit = 1.345


def tables(length):
    period = 2 * length
    frequency = jnp.arange(length + 1, dtype=jnp.int32)
    moment = jnp.arange(length, dtype=jnp.int32)
    phases = frequency[:, None] * moment[None, :] % period
    angles = phases.astype(jnp.float32) * (2.0 * jnp.pi / period)
    cosine = jnp.cos(angles)
    sines = jnp.sin(angles)
    forward = jnp.concatenate([cosine, -sines], 0)
    weight = (
        jnp.where((frequency == 0) | (frequency == length), 1.0, 2.0).astype(jnp.float32) / period
    )
    backward = jnp.concatenate([weight[:, None] * cosine, -weight[:, None] * sines], 0)
    return (forward, backward)


MESH = pl.DeviceIdType.MESH


def remote(src, dst, send, recv, device):
    return pltpu.make_async_remote_copy(
        src_ref=src, dst_ref=dst, send_sem=send, recv_sem=recv, device_id=device, device_id_type=MESH
    )


def residual_kernel(tiles, series, observed, noise, flags, weighted, landed, send_sem, recv_sem):
    sens, par = lax.axis_index("sens"), lax.axis_index("par")
    barrier = pltpu.get_barrier_semaphore()
    for step in range(1, tiles):
        pl.semaphore_signal(
            barrier, inc=1, device_id=(sens, lax.rem(par + step, tiles)), device_id_type=MESH
        )
    pl.semaphore_wait(barrier, tiles - 1)
    copies = []
    for step in range(1, tiles):
        copy = remote(
            series,
            landed.at[step - 1],
            send_sem.at[step - 1],
            recv_sem.at[step - 1],
            (sens, lax.rem(par + step, tiles)),
        )
        copy.start()
        copies.append(copy)
    total = series[...]
    for step, copy in enumerate(copies):
        copy.wait_recv()
        total = total + landed[step]
    deviation = noise[...][None]
    scaled = (total - observed[...][None]) / deviation
    robust = jnp.where(
        flags[...][None] == 1, jnp.clip(scaled, -huber_limit, huber_limit), scaled
    )
    weighted[...] = robust / deviation
    for copy in copies:
        copy.wait_send()


def residual(series, observed, noise_scale, robust_flags):
    tiles = lax.axis_size("par")
    spread = jnp.broadcast_to(noise_scale[:, None], observed.shape)
    return pl.pallas_call(
        functools.partial(residual_kernel, tiles),
        out_shape=jax.ShapeDtypeStruct(series.shape, jnp.float32),
        in_specs=[pl.BlockSpec(memory_space=pltpu.VMEM)] * 4,
        out_specs=pl.BlockSpec(memory_space=pltpu.VMEM),
        scratch_shapes=[
            pltpu.VMEM((tiles - 1,) + series.shape, jnp.float32),
            pltpu.SemaphoreType.DMA((tiles - 1,)),
            pltpu.SemaphoreType.DMA((tiles - 1,)),
        ],
        compiler_params=pltpu.CompilerParams(collective_id=0, has_side_effects=True),
    )(series, observed, spread, robust_flags)


def grid_sum(load, tile, near, inside, rows, chunks):
    lane = lax.broadcasted_iota(jnp.int32, (rows, LANES), 1)
    column = lax.rem(lane, TSIDE)
    west, east, south, north = (near[tile, side] for side in range(4))
    has_west, has_east, has_south, has_north = (inside[tile, side] for side in range(4))
    own = [load(tile, j) for j in range(chunks)]
    up = [pltpu.roll(v, LANES - TSIDE, 1) for v in own]
    up.append(pltpu.roll(load(north, 0), LANES - TSIDE, 1) * has_north)
    down = [pltpu.roll(load(south, chunks - 1), TSIDE, 1) * has_south]
    down += [pltpu.roll(v, TSIDE, 1) for v in own]
    sums = []
    for j in range(chunks):
        east_rim = pltpu.roll(load(east, j), TSIDE - 1, 1) * has_east
        west_rim = pltpu.roll(load(west, j), LANES - TSIDE + 1, 1) * has_west
        east_side = jnp.where(column == TSIDE - 1, east_rim, pltpu.roll(own[j], LANES - 1, 1))
        west_side = jnp.where(column == 0, west_rim, pltpu.roll(own[j], 1, 1))
        north_side = jnp.where(lane < LANES - TSIDE, up[j], up[j + 1])
        south_side = jnp.where(lane >= TSIDE, down[j + 1], down[j])
        sums.append(east_side + west_side + north_side + south_side)
    return sums


def field_kernel(
    groups, tiles, part, param, coef, near, inside, grad_out, dir_out,
    landed, outgoing, misfit, field, coefs, grad, link, inverse, direction, grad_send, dir_send,
    gathered, a_send, a_recv, p_send, p_recv, c_send, c_recv, b_send, b_recv, g_send, g_recv,
    e_send, e_recv,
):
    sens, par = lax.axis_index("sens"), lax.axis_index("par")
    rows, cells = part.shape[1:]
    chunks = cells // LANES
    group_at = [lax.rem(sens + k, groups) for k in range(groups)]
    tile_at = [lax.rem(par + q, tiles) for q in range(tiles)]
    source_at = [lax.rem(par + tiles - q, tiles) for q in range(tiles)]

    barrier = pltpu.get_barrier_semaphore()
    for k in range(1, groups):
        pl.semaphore_signal(barrier, inc=1, device_id=(group_at[k], par), device_id_type=MESH)
    for q in range(1, tiles):
        pl.semaphore_signal(barrier, inc=1, device_id=(sens, tile_at[q]), device_id_type=MESH)
    pl.semaphore_wait(barrier, groups + tiles - 2)

    order = list(range(1, tiles)) + [0]
    a_copies = {}
    for q in order:
        for k in range(1, groups):
            a_copies[k, q] = remote(
                part.at[group_at[k] * tiles + tile_at[q]],
                landed.at[k - 1, q],
                a_send.at[k - 1, q],
                a_recv.at[k - 1, q],
                (group_at[k], par),
            )
            a_copies[k, q].start()
    p_copies = []
    for q in range(1, tiles):
        device = (sens, tile_at[q])
        p_copies.append(
            remote(coef, coefs.at[par], c_send.at[q - 1], c_recv.at[q - 1], device)
        )
        p_copies.append(
            remote(
                param.at[sens * tiles + tile_at[q]],
                field.at[par],
                p_send.at[q - 1],
                p_recv.at[q - 1],
                device,
            )
        )
    for copy in p_copies:
        copy.start()
    field[par] = param[sens * tiles + par]
    coefs[par] = coef[...]

    b_copies = []
    for q in order:
        total = part[sens * tiles + tile_at[q]].astype(jnp.float32)
        for k in range(1, groups):
            a_copies[k, q].wait_recv()
            total = total + landed[k - 1, q].astype(jnp.float32)
        if q == 0:
            misfit[par] = total.astype(jnp.bfloat16)
        else:
            outgoing[q - 1] = total.astype(jnp.bfloat16)
            copy = remote(
                outgoing.at[q - 1],
                misfit.at[par],
                b_send.at[q - 1],
                b_recv.at[q - 1],
                (sens, tile_at[q]),
            )
            copy.start()
            b_copies.append(copy)
    for copy in p_copies:
        copy.wait_recv()

    def spread(tile, carry):
        both = coefs[tile]
        strength, diagonal = both[0:1], both[1:2]
        link[tile] = jnp.broadcast_to(strength, (rows, cells))
        inverse[tile] = jnp.broadcast_to(1.0 / diagonal, (rows, cells))
        for j, total in enumerate(
            grid_sum(lambda i, j: field[i, :, j * LANES : (j + 1) * LANES], tile, near, inside, rows, chunks)
        ):
            at = slice(j * LANES, (j + 1) * LANES)
            grad[tile, :, at] = diagonal[:, at] * field[tile, :, at] - strength[:, at] * total
        return carry

    lax.fori_loop(0, tiles, spread, 0)
    for copy in b_copies:
        copy.wait_recv()

    def add_misfit(tile, carry):
        total = grad[tile] + misfit[tile].astype(jnp.float32)
        grad[tile] = total
        grad_send[tile] = total.astype(jnp.bfloat16)
        direction[0, tile] = total * inverse[tile]
        return carry

    lax.fori_loop(0, tiles, add_misfit, 0)

    def exchange(which, source):
        copies = []
        for q in range(1, tiles):
            copy = remote(
                source.at[tile_at[q]],
                gathered.at[which, sens, par],
                g_send.at[which, q - 1],
                g_recv.at[which, q - 1],
                (sens, tile_at[q]),
            )
            copy.start()
            copies.append(copy)
        gathered[which, sens, par] = source[par]
        return copies

    def forward_on(which, copies):
        onward = []
        for q in range(tiles):
            if q:
                copies[q - 1].wait_recv()
            piece = gathered.at[which, sens, source_at[q]]
            for k in range(1, groups):
                copy = remote(
                    piece,
                    piece,
                    e_send.at[which, k - 1, q],
                    e_recv.at[which, k - 1, q],
                    (group_at[k], par),
                )
                copy.start()
                onward.append(copy)
        return onward

    def sweep(count, carry):
        old, new = lax.rem(count, 2), lax.rem(count + 1, 2)

        def relax(tile, inner):
            sums = grid_sum(
                lambda i, j: direction[old, i, :, j * LANES : (j + 1) * LANES],
                tile, near, inside, rows, chunks,
            )
            for j, total in enumerate(sums):
                at = slice(j * LANES, (j + 1) * LANES)
                direction[new, tile, :, at] = (
                    grad[tile, :, at] + link[tile, :, at] * total
                ) * inverse[tile, :, at]
            return inner

        return lax.fori_loop(0, tiles, relax, carry)

    g_copies = exchange(0, grad_send)
    lax.fori_loop(0, 3, sweep, 0)
    g_onward = forward_on(0, g_copies)
    lax.fori_loop(3, SWEEPS - 1, sweep, 0)

    def pack(tile, carry):
        dir_send[tile] = direction[(SWEEPS - 1) % 2, tile].astype(jnp.bfloat16)
        return carry

    lax.fori_loop(0, tiles, pack, 0)
    d_copies = exchange(1, dir_send)
    d_onward = forward_on(1, d_copies)

    def unpack(which, out):
        def one(index, carry):
            group, tile = index // tiles, lax.rem(index, tiles)
            out[index] = gathered[which, group, tile].astype(jnp.float32)
            return carry

        lax.fori_loop(0, groups * tiles, one, 0)

    for copy in g_onward:
        copy.wait_recv()
    unpack(0, grad_out)
    for copy in d_onward:
        copy.wait_recv()
    unpack(1, dir_out)
    for copy in list(a_copies.values()) + p_copies + b_copies + g_copies + d_copies + g_onward + d_onward:
        copy.wait_send()


def field_stage(part, param, coef, neighbours):
    groups, tiles = lax.axis_size("sens"), lax.axis_size("par")
    rows, cells = part.shape[1:]
    f32, bf16 = jnp.float32, jnp.bfloat16
    near = jnp.maximum(neighbours, 0)
    inside = (neighbours >= 0).astype(f32)
    full = jax.ShapeDtypeStruct(param.shape, f32)
    dma = pltpu.SemaphoreType.DMA
    block = (tiles, rows, cells)
    vmem, smem = pl.BlockSpec(memory_space=pltpu.VMEM), pl.BlockSpec(memory_space=pltpu.SMEM)
    sems = [(groups - 1, tiles), (tiles - 1,), (tiles - 1,), (tiles - 1,), (2, tiles - 1), (2, groups - 1, tiles)]
    return pl.pallas_call(
        functools.partial(field_kernel, groups, tiles),
        out_shape=(full, full),
        in_specs=[vmem, vmem, vmem, smem, smem],
        out_specs=(vmem, vmem),
        scratch_shapes=[
            pltpu.VMEM((groups - 1,) + block, bf16),
            pltpu.VMEM((tiles - 1, rows, cells), bf16),
            pltpu.VMEM(block, bf16),
            pltpu.VMEM(block, f32),
            pltpu.VMEM((tiles, 2, cells), f32),
            pltpu.VMEM(block, f32),
            pltpu.VMEM(block, f32),
            pltpu.VMEM(block, f32),
            pltpu.VMEM((2,) + block, f32),
            pltpu.VMEM(block, bf16),
            pltpu.VMEM(block, bf16),
            pltpu.VMEM((2, groups) + block, bf16),
        ]
        + [dma(shape) for shape in sems for _ in range(2)],
        compiler_params=pltpu.CompilerParams(collective_id=1, has_side_effects=True),
    )(part, param, coef, near, inside)


def per_device(
    kernel, param, observed, noise_scale, robust_flags, kappa_field, coupling, neighbours
):
    length, samples, cell_count = param.shape
    sensor_count = observed.shape[0]
    spectra_rows = 2 * (length + 1)
    forward, backward = tables(length)
    spectrum = jnp.dot(forward, param.reshape(length, -1), precision=lax.Precision.HIGHEST)
    spectrum = spectrum.reshape(2, length + 1, samples, cell_count).astype(jnp.bfloat16)
    product = jnp.einsum("ifsc,jfbc->ijfsb", kernel, spectrum, preferred_element_type=jnp.float32)
    partial_sum = jnp.concatenate([product[0, 0] - product[1, 1], product[0, 1] + product[1, 0]], 0)
    series = jnp.einsum("ft,fsb->bst", backward, partial_sum, precision=lax.Precision.HIGHEST)
    weighted = residual(series, observed, noise_scale, robust_flags)
    adjoint = jnp.einsum("ft,bst->fsb", backward, weighted, precision=lax.Precision.HIGHEST)
    adjoint = adjoint.astype(jnp.bfloat16).reshape(2, length + 1, sensor_count, samples)
    back_product = jnp.einsum(
        "ifsc,jfsb->ijfbc", kernel, adjoint, preferred_element_type=jnp.float32
    )
    partial_grad = jnp.concatenate(
        [back_product[0, 0] + back_product[1, 1], back_product[0, 1] - back_product[1, 0]], 0
    )
    partial_grad = partial_grad.reshape(spectra_rows, samples * cell_count)
    misfit = jnp.dot(forward.T, partial_grad, precision=lax.Precision.HIGHEST)
    devices = lax.axis_size("sens") * lax.axis_size("par")
    blocks = (devices, length * samples // devices, cell_count)
    coef = jnp.stack([coupling, kappa_field + 4.0 * coupling], 0)
    gradient, direction = field_stage(
        misfit.astype(jnp.bfloat16).reshape(blocks), param.reshape(blocks), coef, neighbours
    )
    return gradient.reshape(param.shape), direction.reshape(param.shape)


def solution(mesh):
    return jax.shard_map(
        per_device,
        mesh=mesh,
        in_specs=(
            P(None, None, "sens", "par"),
            P(None, None, "par"),
            P("sens", None),
            P("sens"),
            P("sens", None),
            P("par"),
            P("par"),
            P(),
        ),
        out_specs=(P(None, None, "par"), P(None, None, "par")),
        check_vma=False,
    )
```

time: 280 us -> 91.3 us (0.33)
  blocking collectives: 143 us -> 0 us
  waiting for transfers between devices: 56.5 us -> 0 us
  Pallas kernels: 0 us -> 49.3 us
  between operations: 20.3 us -> 0.81 us
  local copies, waits for them, and re-layouts: 28.3 us -> 11.8 us
  other arithmetic: 6.71 us -> 3.65 us
    all_gather x8 -> x0, blocking collectives: 112 us -> none  [neighbour_sum(): lax.all_gather(outgoing.astype(jnp.bfloat16), 'par', axis=0, tiled=True)]
    all_gather x2 -> x0, waiting for transfers between devices: 54.5 us -> none  [the longest x1 28.9 us: per_device(): lax.all_gather(gradient, 'sens', axis=0, tiled=True)]
    pallas_call x0 -> x2, Pallas kernels: none -> 49.3 us  [the longest x1 39.5 us: field_stage(): pl.pallas_call(functools.partial(field_kernel, groups, tiles), out_shape=...]
    psum x1 -> x0, blocking collectives: 30.7 us -> none  [per_device(): predicted = lax.psum(partial_sum, 'par')]
    slice x61 -> x0, local copies, waits for them, and re-layouts: 6.67 us -> none  [the longest x15 1.69 us: neighbour_sum(): square[:, :, 0]]
    another operation x40 -> x0, local copies, waits for them, and re-layouts: 4.37 us -> none  [the longest x32 2.93 us: neighbour_sum(): jnp.stack([square[:, :, 0], square[:, :, -1], square[:, 0, :], square[:,...]
    select_n x48 -> x0, local copies, waits for them, and re-layouts: 3.36 us -> none  [facing(): return jnp.where(tile >= 0, picked, 0.0).reshape(row_count, TSIDE)]
    unnamed x21 -> x18, local copies, waits for them, and re-layouts: 6.34 us -> 3.17 us
  transfers between devices with their start and end apart: 3 -> 0, of which waited for: 3 -> 0; matrix products, arithmetic and copies ran while one was open for 2% -> 0% of each run, Pallas kernels for 0% -> 0%
where the time goes in v1:
time: 91.3 us; the launch traced here: 90.9 us
  Pallas kernels  49.3 us (54%)
  matrix products  25.3 us (28%)
  local copies, waits for them, and re-layouts  11.8 us (13%)
  other arithmetic  3.65 us (4%)
    pallas_call x1, Pallas kernels, field_stage(): pl.pallas_call(functools.partial(field_kernel, groups, tiles), out_shape=...  39.5 us
    dot_general x1, matrix products, per_device(): jnp.einsum('ifsc,jfbc->ijfsb', kernel, spectrum, preferred_element_type=j...  13.9 us
    pallas_call x1, Pallas kernels, residual(): pl.pallas_call(functools.partial(residual_kernel, tiles), out_shape=jax.S...  9.8 us
    dot_general x1, matrix products, per_device(): jnp.einsum('ifsc,jfsb->ijfbc', kernel, adjoint, preferred_element_type=jn...  5.6 us
    reshape x2, local copies, waits for them, and re-layouts, per_device(): return (gradient.reshape(param.shape), direction.reshape(param.shape))  4.49 us
    unnamed x18, local copies, waits for them, and re-layouts  3.17 us
    dot_general x1, matrix products, per_device(): misfit = jnp.dot(forward.T, partial_grad, precision=lax.Precision.HIGHEST)  2.07 us
    dot_general x1, matrix products, per_device(): jnp.dot(forward, param.reshape(length, -1), precision=lax.Precision.HIGHEST)  1.91 us

profile of v1, /device:TPU:0, one launch (start us, length us, event | category | flops | bytes accessed | tf_op | source)
XLA Modules:
  0.0 90.9 jit_solution(9202433896440774878)
XLA Ops:
  0.6 0.3 fusion.31
  1.0 1.6 %copy.46 = f32[16,8,2,1024]{3,1,2,0:T(8,128)S(1)} copy(f32[16,8,2,1024]{3,2,1,0:T(2,128)} %bitcast.61) | data formatting | bytes 2097152
  2.5 0.3 copy.24
  2.9 1.9 %fusion.10 = bf16[2,129,2,1024,1]{3,1,2,0,4:T(8,128)(2,1)S(1)} fusion(f32[2,1024,128,1]{2,1,0,3:T(8,128)S(1)} %bitcast.62, f32[2,129,128,1]{2,1,0,3:T(8,128)S(1)} %reshape.56), kind=kOutput, calls=%fused_computation.10 | convolution fusion | flops 812126208 | bytes 2237440 | tf_op jit(solution)/shard_map/dot_general | solution.py:337
  4.8 13.9 %fusion.11 = f32[2,2,129,16,2]{3,4,0,1,2:T(2,128)S(1)} fusion(bf16[2,129,2,1024,1]{3,1,2,0,4:T(8,128)(2,1)S(1)} %fusion.10, bf16[2,129,16,1024]{3,2,1,0:T(8,128)(2,1)} %param.8), kind=kOutput, calls=%fused_computation.11 | convolution fusion | flops 33816576 | bytes 9576960 | tf_op jit(solution)/shard_map/ifsc,jfbc->ijfsb/dot_general | solution.py:339
  18.7 0.0 copy-start.5
  18.7 0.1 fusion.20
  18.8 0.1 copy.27
  18.9 0.1 copy.28
  19.1 0.3 broadcast_multiply_fusion
  19.4 0.9 convolution_bitcast_fusion.series
  20.2 0.0 copy-done.5
  20.2 0.7 broadcast_in_dim.20.noise
  20.9 9.8 %shard_map.95 = f32[2,16,128]{2,1,0:T(8,128)} custom-call(f32[2,16,128]{2,1,0:T(8,128)} %convolution_bitcast_fusion.series, f32[16,128]{1,0:T(8,128)} %observed.1, f32[16,128]{1,0:T(8,128)} %broadcast_in_dim.20.noise, s32[16,128]{1,0:T(8,128)} %flags.1), custom_call_target="tpu_custom_call" | custom-call | tf_op jit(solution)/shard_map/pallas_call | solution.py:79
  30.7 1.0 %fusion.14 = bf16[258,16,2]{0,1,2:T(8,128)(2,1)S(1)} fusion(f32[2,16,128]{2,1,0:T(8,128)} %shard_map.95, f32[129,128]{1,0:T(8,128)S(1)} %get-tuple-element.12, f32[129,128]{1,0:T(8,128)S(1)} %get-tuple-element.13), kind=kOutput, calls=%fused_computation.13 | convolution fusion | flops 12722496 | bytes 164992 | tf_op jit(solution)/shard_map/ft,bst->fsb/dot_general | solution.py:343
  31.7 0.1 reshape.51
  31.8 0.2 copy.36
  32.0 5.6 %fusion.4 = f32[2,2,129,2,1024]{4,3,0,1,2:T(2,128)S(1)} fusion(bf16[2,129,16,2,1]{2,3,4,0,1:T(2,128)(2,1)S(1)} %copy.36, bf16[2,129,16,1024]{3,2,1,0:T(8,128)(2,1)} %param.8), kind=kOutput, calls=%fused_computation.4 | convolution fusion | flops 33816576 | bytes 12697728 | tf_op jit(solution)/shard_map/ifsc,jfsb->ijfbc/dot_general | solution.py:345
  37.6 1.1 %fusion.16 = (f32[129,2,1024]{2,1,0:T(2,128)S(1)}, f32[129,2,1024]{2,1,0:T(2,128)S(1)}) fusion(f32[2,2,129,2,1024]{4,3,0,1,2:T(2,128)S(1)} %fusion.4), kind=kLoop, calls=%fused_computation.18 | loop fusion | flops 528384 | bytes 6340608
  38.7 0.4 pad.10
  39.1 0.4 copy.47
  39.5 0.4 pad.11
  39.8 0.4 copy.48
  40.2 0.0 copy-start.4
  40.2 2.1 %convolution_convert_fusion = bf16[128,2048]{1,0:T(8,128)(2,1)S(1)} fusion(f32[258,128]{1,0:T(8,128)S(1)} %pad_maximum_fusion, f32[129,2048]{1,0:T(8,128)S(1)} %bitcast.60, f32[129,2048]{1,0:T(8,128)S(1)} %bitcast.59), kind=kOutput, calls=%fused_computation.5 | convolution fusion | flops 812388352 | bytes 2769920 | tf_op jit(solution)/shard_map/dot_general | solution.py:352
  42.3 0.0 copy-start
  42.3 1.0 %reshape.52.part = bf16[32,8,1024]{2,1,0:T(8,128)(2,1)} reshape(bf16[128,2048]{1,0:T(8,128)(2,1)S(1)} %convolution_convert_fusion) | data formatting | bytes 1048576 | tf_op jit(solution)/shard_map/reshape | solution.py:357
  43.3 0.0 copy-done.4
  43.3 0.0 copy-start.2
  43.3 0.0 copy-start.3
  43.3 0.1 copy.31
  43.4 0.6 broadcast_maximum_fusion.near
  44.0 0.6 compare_convert_fusion.inside
  44.6 0.0 copy-done
  44.6 1.7 %reshape.53.param = f32[32,8,1024]{2,1,0:T(8,128)} reshape(f32[128,2,1024]{2,1,0:T(2,128)S(1)} %copy-done) | data formatting | bytes 2097152 | tf_op jit(solution)/shard_map/reshape | solution.py:357
  46.3 0.0 copy-done.2
  46.3 0.0 copy-done.3
  46.3 0.6 pad_maximum_fusion.1.coef
  46.9 39.5 %shard_map.96 = (f32[32,8,1024]{2,1,0:T(8,128)}, f32[32,8,1024]{2,1,0:T(8,128)}) custom-call(bf16[32,8,1024]{2,1,0:T(8,128)(2,1)} %reshape.52.part, f32[32,8,1024]{2,1,0:T(8,128)} %reshape.53.param, f32[2,1024]{1,0:T(2,128)} %pad_maximum_fusion.1.coef, s32[8,4]{1,0:T(8,128)} %broadcast_maximum_fusion.near, f32[8,4]{1,0:T(8,128)} %compare_convert_fusion.inside), custom_call_target="tpu_custom_call" | custom-call | tf_op jit(solution)/shard_map/pallas_call | solution.py:306
  86.4 0.0 copy-start.1
  86.4 2.9 %reshape.54 = f32[128,2,1024]{2,1,0:T(2,128)} reshape(f32[32,8,1024]{2,1,0:T(8,128)} %get-tuple-element.4) | data formatting | bytes 2097152 | tf_op jit(solution)/shard_map/reshape | solution.py:359
  89.3 0.0 copy-done.1
  89.3 1.6 %reshape.55 = f32[128,2,1024]{2,1,0:T(2,128)} reshape(f32[32,8,1024]{2,1,0:T(8,128)S(1)} %copy-done.1) | data formatting | bytes 2097152 | tf_op jit(solution)/shard_map/reshape | solution.py:359
  (5 shorter events, 0.0 us)
Async XLA Ops:
  18.7 1.6 %copy-start.5 = (f32[16]{0:T(128)S(1)}, f32[16]{0:T(128)}, u32[]{:S(2)}) copy-start(f32[16]{0:T(128)} %param.11) | copy-start | bytes 196
  40.2 3.1 %copy-start.4 = (s32[8,4]{0,1:T(4,128)S(1)}, s32[8,4]{0,1:T(4,128)}, u32[]{:S(2)}) copy-start(s32[8,4]{0,1:T(4,128)} %param.15) | copy-start | bytes 388
  42.3 2.3 %copy-start = (f32[128,2,1024]{2,1,0:T(2,128)S(1)}, f32[128,2,1024]{2,1,0:T(2,128)}, u32[]{:S(2)}) copy-start(f32[128,2,1024]{2,1,0:T(2,128)} %param.9) | copy-start | bytes 3145732
  43.3 3.0 %copy-start.2 = (f32[1024]{0:T(1024)S(1)}, f32[1024]{0:T(1024)}, u32[]{:S(2)}) copy-start(f32[1024]{0:T(1024)} %param.14) | copy-start | bytes 12292
  43.3 3.0 %copy-start.3 = (f32[1024]{0:T(1024)S(1)}, f32[1024]{0:T(1024)}, u32[]{:S(2)}) copy-start(f32[1024]{0:T(1024)} %param.13) | copy-start | bytes 12292
  86.4 2.9 %copy-start.1 = (f32[32,8,1024]{2,1,0:T(8,128)S(1)}, f32[32,8,1024]{2,1,0:T(8,128)}, u32[]{:S(2)}) copy-start(f32[32,8,1024]{2,1,0:T(8,128)} %get-tuple-element.5) | copy-start | bytes 3145732

commit v2 on v1

--- a/solution.py
+++ b/solution.py
@@ -63,10 +63,10 @@
     for step, copy in enumerate(copies):
         copy.wait_recv()
         total = total + landed[step]
-    deviation = noise[...][None]
-    scaled = (total - observed[...][None]) / deviation
+    deviation = noise[...]
+    scaled = (total - observed[...]) / deviation
     robust = jnp.where(
-        flags[...][None] == 1, jnp.clip(scaled, -huber_limit, huber_limit), scaled
+        flags[...] == 1, jnp.clip(scaled, -huber_limit, huber_limit), scaled
     )
     weighted[...] = robust / deviation
     for copy in copies:
@@ -90,11 +90,14 @@
     )(series, observed, spread, robust_flags)
 
 
-def grid_sum(load, tile, near, inside, rows, chunks):
+def grid_sum(load, tile, near, rows, chunks):
     lane = lax.broadcasted_iota(jnp.int32, (rows, LANES), 1)
     column = lax.rem(lane, TSIDE)
-    west, east, south, north = (near[tile, side] for side in range(4))
-    has_west, has_east, has_south, has_north = (inside[tile, side] for side in range(4))
+    beside = [near[tile, side] for side in range(4)]
+    west, east, south, north = (jnp.maximum(index, 0) for index in beside)
+    has_west, has_east, has_south, has_north = (
+        jnp.minimum(index + 1, 1).astype(jnp.float32) for index in beside
+    )
     own = [load(tile, j) for j in range(chunks)]
     up = [pltpu.roll(v, LANES - TSIDE, 1) for v in own]
     up.append(pltpu.roll(load(north, 0), LANES - TSIDE, 1) * has_north)
@@ -113,7 +116,7 @@
 
 
 def field_kernel(
-    groups, tiles, part, param, coef, near, inside, grad_out, dir_out,
+    groups, tiles, part, param, coef, near, grad_out, dir_out,
     landed, outgoing, misfit, field, coefs, grad, link, inverse, direction, grad_send, dir_send,
     gathered, a_send, a_recv, p_send, p_recv, c_send, c_recv, b_send, b_recv, g_send, g_recv,
     e_send, e_recv,
@@ -171,9 +174,9 @@
             a_copies[k, q].wait_recv()
             total = total + landed[k - 1, q].astype(jnp.float32)
         if q == 0:
-            misfit[par] = total.astype(jnp.bfloat16)
+            misfit[par] = total
         else:
-            outgoing[q - 1] = total.astype(jnp.bfloat16)
+            outgoing[q - 1] = total
             copy = remote(
                 outgoing.at[q - 1],
                 misfit.at[par],
@@ -192,7 +195,7 @@
         link[tile] = jnp.broadcast_to(strength, (rows, cells))
         inverse[tile] = jnp.broadcast_to(1.0 / diagonal, (rows, cells))
         for j, total in enumerate(
-            grid_sum(lambda i, j: field[i, :, j * LANES : (j + 1) * LANES], tile, near, inside, rows, chunks)
+            grid_sum(lambda i, j: field[i, :, j * LANES : (j + 1) * LANES], tile, near, rows, chunks)
         ):
             at = slice(j * LANES, (j + 1) * LANES)
             grad[tile, :, at] = diagonal[:, at] * field[tile, :, at] - strength[:, at] * total
@@ -203,7 +206,7 @@
         copy.wait_recv()
 
     def add_misfit(tile, carry):
-        total = grad[tile] + misfit[tile].astype(jnp.float32)
+        total = grad[tile] + misfit[tile]
         grad[tile] = total
         grad_send[tile] = total.astype(jnp.bfloat16)
         direction[0, tile] = total * inverse[tile]
@@ -250,7 +253,7 @@
         def relax(tile, inner):
             sums = grid_sum(
                 lambda i, j: direction[old, i, :, j * LANES : (j + 1) * LANES],
-                tile, near, inside, rows, chunks,
+                tile, near, rows, chunks,
             )
             for j, total in enumerate(sums):
                 at = slice(j * LANES, (j + 1) * LANES)
@@ -296,8 +299,6 @@
     groups, tiles = lax.axis_size("sens"), lax.axis_size("par")
     rows, cells = part.shape[1:]
     f32, bf16 = jnp.float32, jnp.bfloat16
-    near = jnp.maximum(neighbours, 0)
-    inside = (neighbours >= 0).astype(f32)
     full = jax.ShapeDtypeStruct(param.shape, f32)
     dma = pltpu.SemaphoreType.DMA
     block = (tiles, rows, cells)
@@ -306,12 +307,12 @@
     return pl.pallas_call(
         functools.partial(field_kernel, groups, tiles),
         out_shape=(full, full),
-        in_specs=[vmem, vmem, vmem, smem, smem],
+        in_specs=[vmem, vmem, vmem, smem],
         out_specs=(vmem, vmem),
         scratch_shapes=[
             pltpu.VMEM((groups - 1,) + block, bf16),
-            pltpu.VMEM((tiles - 1, rows, cells), bf16),
-            pltpu.VMEM(block, bf16),
+            pltpu.VMEM((tiles - 1, rows, cells), f32),
+            pltpu.VMEM(block, f32),
             pltpu.VMEM(block, f32),
             pltpu.VMEM((tiles, 2, cells), f32),
             pltpu.VMEM(block, f32),
@@ -324,38 +325,151 @@
         ]
         + [dma(shape) for shape in sems for _ in range(2)],
         compiler_params=pltpu.CompilerParams(collective_id=1, has_side_effects=True),
-    )(part, param, coef, near, inside)
+    )(part, param, coef, neighbours)
+
+
+HIGH = lax.Precision.HIGHEST
+LAST = (((1,), (1,)), ((), ()))
+
+
+def block_tables(length, samples):
+    forward, backward = tables(length)
+    count = length + 1
+    size = max(d for d in range(1, 65) if count % d == 0)
+    padded = -(-size // 4) * 4
+    blocks = count // size
+    eye = jnp.eye(samples, dtype=jnp.float32)
+
+    def arrange(table):
+        table = table.reshape(2, blocks, size, length)
+        return jnp.pad(table, ((0, 0), (0, 0), (0, padded - size), (0, 0)))
+
+    fore, back = arrange(forward), arrange(backward)
+    turned = jnp.stack([back[1], -back[0]], 0)
+    rows = samples * 2 * padded
+    fields = jnp.einsum("jkft,bd->kbjftd", fore, eye).reshape(blocks, rows, -1)
+    sensors = [
+        jnp.einsum("jkft,bd->kbjfdt", table, eye).reshape(blocks, rows, -1)
+        for table in (back, turned)
+    ]
+    return fields, jnp.stack(sensors, 1), size, padded
+
+
+def diagonal(shape, width, padded, frequency_dim):
+    own = lax.broadcasted_iota(jnp.int32, shape, frequency_dim)
+    other = lax.broadcasted_iota(jnp.int32, shape, 1 - frequency_dim)
+    return own // width == lax.rem(other, padded)
+
+
+def predict_kernel(padded, kernel, param, fields, sensors, series):
+    size, sensor_count, cells = kernel.shape[1:]
+    spectrum = jnp.dot(fields[0], param[...], precision=HIGH, preferred_element_type=jnp.float32)
+    spectrum = spectrum.astype(jnp.bfloat16)
+    total = jnp.zeros(series.shape, jnp.float32)
+    for i in range(2):
+        product = lax.dot_general(
+            kernel[i].reshape(size * sensor_count, cells),
+            spectrum,
+            LAST,
+            preferred_element_type=jnp.float32,
+        )
+        product = jnp.where(diagonal(product.shape, sensor_count, padded, 0), product, 0.0)
+        timed = jnp.dot(product, sensors[0, i], precision=HIGH, preferred_element_type=jnp.float32)
+        total = total + jnp.sum(timed.reshape(size, sensor_count, -1), 0)
+
+    @pl.when(pl.program_id(0) == 0)
+    def _():
+        series[...] = jnp.zeros_like(series)
+
+    series[...] += total
+
+
+def predict(kernel, param, fields, sensors, size, padded):
+    blocks, rows, width = fields.shape
+    sensor_count, cells = kernel.shape[2:]
+    return pl.pallas_call(
+        functools.partial(predict_kernel, padded),
+        out_shape=jax.ShapeDtypeStruct((sensor_count, width), jnp.float32),
+        grid=(blocks,),
+        in_specs=[
+            pl.BlockSpec((2, size, sensor_count, cells), lambda k: (0, k, 0, 0)),
+            pl.BlockSpec(param.shape, lambda k: (0, 0)),
+            pl.BlockSpec((1, rows, width), lambda k: (k, 0, 0)),
+            pl.BlockSpec((1, 2, rows, width), lambda k: (k, 0, 0, 0)),
+        ],
+        out_specs=pl.BlockSpec((sensor_count, width), lambda k: (0, 0)),
+    )(kernel, param, fields, sensors)
+
+
+def backward_kernel(padded, blocks, kernel, weighted, fields, sensors, part, total):
+    size, sensor_count, cells = kernel.shape[1:]
+    rows = sensors.shape[2]
+    pairs = size * sensor_count
+    copies = lax.rem(lax.broadcasted_iota(jnp.int32, (sensor_count, pairs), 1), sensor_count)
+    copies = copies == lax.broadcasted_iota(jnp.int32, (sensor_count, pairs), 0)
+    copies = jnp.where(copies, 1.0, 0.0).astype(jnp.bfloat16)
+    keep = diagonal((rows, pairs), sensor_count, padded, 1)
+    back = jnp.zeros((rows, cells), jnp.float32)
+    for i in range(2):
+        adjoint = lax.dot_general(
+            sensors[0, i], weighted[...], LAST, precision=HIGH, preferred_element_type=jnp.float32
+        )
+        wide = jnp.dot(adjoint.astype(jnp.bfloat16), copies, preferred_element_type=jnp.float32)
+        wide = jnp.where(keep, wide, 0.0).astype(jnp.bfloat16)
+        back = back + jnp.dot(
+            wide, kernel[i].reshape(pairs, cells), preferred_element_type=jnp.float32
+        )
+    misfit = jnp.dot(fields[0], back, precision=HIGH, preferred_element_type=jnp.float32)
+
+    @pl.when(pl.program_id(0) == 0)
+    def _():
+        total[...] = jnp.zeros_like(total)
+
+    total[...] += misfit
+
+    @pl.when(pl.program_id(0) == blocks - 1)
+    def _():
+        part[...] = total[...].reshape(part.shape).astype(part.dtype)
+
+
+def back_project(kernel, weighted, fields, sensors, size, padded, shape):
+    blocks, width, rows = fields.shape
+    sensor_count, cells = kernel.shape[2:]
+    return pl.pallas_call(
+        functools.partial(backward_kernel, padded, blocks),
+        out_shape=jax.ShapeDtypeStruct(shape, jnp.bfloat16),
+        grid=(blocks,),
+        in_specs=[
+            pl.BlockSpec((2, size, sensor_count, cells), lambda k: (0, k, 0, 0)),
+            pl.BlockSpec(weighted.shape, lambda k: (0, 0)),
+            pl.BlockSpec((1, width, rows), lambda k: (k, 0, 0)),
+            pl.BlockSpec((1, 2, rows, weighted.shape[1]), lambda k: (k, 0, 0, 0)),
+        ],
+        out_specs=pl.BlockSpec(shape, lambda k: (0, 0, 0)),
+        scratch_shapes=[pltpu.VMEM((width, cells), jnp.float32)],
+    )(kernel, weighted, fields, sensors)
 
 
 def per_device(
     kernel, param, observed, noise_scale, robust_flags, kappa_field, coupling, neighbours
 ):
     length, samples, cell_count = param.shape
-    sensor_count = observed.shape[0]
-    spectra_rows = 2 * (length + 1)
-    forward, backward = tables(length)
-    spectrum = jnp.dot(forward, param.reshape(length, -1), precision=lax.Precision.HIGHEST)
-    spectrum = spectrum.reshape(2, length + 1, samples, cell_count).astype(jnp.bfloat16)
-    product = jnp.einsum("ifsc,jfbc->ijfsb", kernel, spectrum, preferred_element_type=jnp.float32)
-    partial_sum = jnp.concatenate([product[0, 0] - product[1, 1], product[0, 1] + product[1, 0]], 0)
-    series = jnp.einsum("ft,fsb->bst", backward, partial_sum, precision=lax.Precision.HIGHEST)
-    weighted = residual(series, observed, noise_scale, robust_flags)
-    adjoint = jnp.einsum("ft,bst->fsb", backward, weighted, precision=lax.Precision.HIGHEST)
-    adjoint = adjoint.astype(jnp.bfloat16).reshape(2, length + 1, sensor_count, samples)
-    back_product = jnp.einsum(
-        "ifsc,jfsb->ijfbc", kernel, adjoint, preferred_element_type=jnp.float32
-    )
-    partial_grad = jnp.concatenate(
-        [back_product[0, 0] + back_product[1, 1], back_product[0, 1] - back_product[1, 0]], 0
-    )
-    partial_grad = partial_grad.reshape(spectra_rows, samples * cell_count)
-    misfit = jnp.dot(forward.T, partial_grad, precision=lax.Precision.HIGHEST)
+    fields, sensors, size, padded = block_tables(length, samples)
     devices = lax.axis_size("sens") * lax.axis_size("par")
     blocks = (devices, length * samples // devices, cell_count)
+    flat = param.reshape(length * samples, cell_count)
+    series = predict(kernel, flat, fields, sensors, size, padded)
+    weighted = residual(
+        series,
+        jnp.tile(observed, (1, samples)),
+        noise_scale,
+        jnp.tile(robust_flags, (1, samples)),
+    )
+    part = back_project(
+        kernel, weighted, fields.transpose(0, 2, 1), sensors, size, padded, blocks
+    )
     coef = jnp.stack([coupling, kappa_field + 4.0 * coupling], 0)
-    gradient, direction = field_stage(
-        misfit.astype(jnp.bfloat16).reshape(blocks), param.reshape(blocks), coef, neighbours
-    )
+    gradient, direction = field_stage(part, flat.reshape(blocks), coef, neighbours)
     return gradient.reshape(param.shape), direction.reshape(param.shape)
 
 

time: 91.3 us -> 111 us (1.22)
  Pallas kernels: 49.3 us -> 81.6 us
  matrix products: 25.3 us -> 0 us
  local copies, waits for them, and re-layouts: 11.8 us -> 23.2 us
  other arithmetic: 3.65 us -> 5.29 us
    pallas_call x0 -> x2, Pallas kernels: none -> 29.3 us  [the longest x1 18.7 us: predict(): pl.pallas_call(functools.partial(predict_kernel, padded), out_shape=jax.S...]
    dot_general x6 -> x0, matrix products: 25.3 us -> none  [the longest x1 13.9 us: per_device(): jnp.einsum('ifsc,jfbc->ijfsb', kernel, spectrum, preferred_element_type=j...]
    transpose x0 -> x2, local copies, waits for them, and re-layouts: none -> 5.05 us  [block_tables(): jnp.einsum('jkft,bd->kbjfdt', table, eye).reshape(blocks, rows, -1)]
    another operation x0 -> x7, local copies, waits for them, and re-layouts: none -> 4.92 us  [the longest x3 3 us: block_tables(): return (fields, jnp.stack(sensors, 1), size, padded)]
    transpose x0 -> x1, other arithmetic: none -> 4.02 us  [block_tables(): jnp.einsum('jkft,bd->kbjfdt', table, eye).reshape(blocks, rows, -1)]
    pallas_call x1, Pallas kernels: 39.5 us -> 42.5 us  [field_stage(): pl.pallas_call(functools.partial(field_kernel, groups, tiles), out_shape=...]
    reshape x4 -> x5, local copies, waits for them, and re-layouts: 2.91 us -> 4 us  [the longest x2 2.29 us: block_tables(): fields = jnp.einsum('jkft,bd->kbjftd', fore, eye).reshape(blocks, rows, -1)]
    unnamed x18 -> x26, local copies, waits for them, and re-layouts: 3.17 us -> 3.02 us
where the time goes in v2:
time: 111 us
  Pallas kernels  81.6 us (74%)
  local copies, waits for them, and re-layouts  23.2 us (21%)
  other arithmetic  5.29 us (5%)
    pallas_call x1, Pallas kernels, field_stage(): pl.pallas_call(functools.partial(field_kernel, groups, tiles), out_shape=...  42.5 us
    pallas_call x1, Pallas kernels, predict(): pl.pallas_call(functools.partial(predict_kernel, padded), out_shape=jax.S...  18.7 us
    pallas_call x1, Pallas kernels, back_project(): pl.pallas_call(functools.partial(backward_kernel, padded, blocks), out_sh...  10.6 us
    pallas_call x1, Pallas kernels, residual(): pl.pallas_call(functools.partial(residual_kernel, tiles), out_shape=jax.S...  9.82 us
    transpose x2, local copies, waits for them, and re-layouts, block_tables(): jnp.einsum('jkft,bd->kbjfdt', table, eye).reshape(blocks, rows, -1)  5.05 us
    reshape x2, local copies, waits for them, and re-layouts, per_device(): return (gradient.reshape(param.shape), direction.reshape(param.shape))  4.49 us
    transpose x1, other arithmetic, block_tables(): jnp.einsum('jkft,bd->kbjfdt', table, eye).reshape(blocks, rows, -1)  4.02 us
    unnamed x26, local copies, waits for them, and re-layouts  3.02 us

profile of v2, /device:TPU:0, one launch (start us, length us, event | category | flops | bytes accessed | tf_op | source)
XLA Modules:
  0.0 110.9 jit_solution(16794061807530512127)
XLA Ops:
  0.7 0.3 broadcast_multiply_fusion
  1.0 0.2 copy.16
  1.3 0.2 copy.25
  1.5 0.9 pad.8.clone
  2.4 0.3 fusion.7
  2.7 0.2 copy.20
  2.9 0.1 pad.7.clone
  3.1 4.0 %multiply_bitcast_fusion = (f32[3,2,2,44,2,128]{3,2,1,4,5,0:T(2,128)}, f32[3,2,2,44,2,128]{3,2,1,4,5,0:T(2,128)S(1)}, f32[3,2,2,44,128,2]{3,2,1,5,4,0:T(2,128)S(1)}) fusion(f32[2,3,44,128]{2,0,3,1:T(2,128)S(1)} %copy.16, f32[2,2]{0,1:T(2,128)S(1)} %compare_convert_fusion, f32[2,3,44,128]{2,0,3,1:T(2,128)} %pad.8.clone, f32[2,3,44,128]{2,0,3,1:T(2,128)S(1)} %pad.7.clone), kind=kLoop, calls=%fused_computation | loop fusion | flops 405504 | bytes 2027536 | tf_op jit(solution)/shard_map/jkft,bd->kbjfdt/transpose | solution.py:352
  7.1 1.8 %copy.15 = f32[3,2,2,44,2,128]{5,4,3,2,1,0:T(2,128)} copy(f32[3,2,2,44,2,128]{3,2,1,4,5,0:T(2,128)S(1)} %get-tuple-element.9) | data formatting | bytes 1081344 | tf_op jit(solution)/shard_map/jkft,bd->kbjfdt/transpose | solution.py:352
  8.9 1.5 %stack_reshape.6 = f32[3,1,176,256]{3,2,1,0:T(8,128)S(1)} reshape(f32[3,2,2,44,2,128]{5,4,3,2,1,0:T(2,128)} %copy.15) | data formatting | bytes 1081344 | tf_op jit(solution)/shard_map/stack;reshape | solution.py:355
  10.5 3.2 %copy.17 = f32[3,2,2,44,2,128]{5,4,3,2,1,0:T(2,128)} copy(f32[3,2,2,44,2,128]{3,2,1,4,5,0:T(2,128)} %get-tuple-element.8) | data formatting | bytes 1081344 | tf_op jit(solution)/shard_map/jkft,bd->kbjfdt/transpose | solution.py:352
  13.7 1.5 %stack_reshape.7 = f32[3,1,176,256]{3,2,1,0:T(8,128)S(1)} reshape(f32[3,2,2,44,2,128]{5,4,3,2,1,0:T(2,128)} %copy.17) | data formatting | bytes 1081344 | tf_op jit(solution)/shard_map/stack;reshape | solution.py:355
  15.2 0.0 copy-start.1
  15.2 1.2 %reshape.46 = f32[3,176,256]{1,2,0:T(8,128)S(1)} reshape(f32[3,2,2,44,128,2]{3,2,1,5,4,0:T(2,128)S(1)} %get-tuple-element.10) | data formatting | bytes 1081344 | tf_op jit(solution)/shard_map/reshape | solution.py:350
  16.4 0.0 copy-start
  16.5 0.0 copy-start.2
  16.5 1.1 copy.18.fields
  17.5 0.0 copy-done.1
  17.5 0.6 copy-done.2
  18.2 1.7 %reshape.44.param = f32[256,1024]{1,0:T(8,128)} reshape(f32[128,2,1024]{2,1,0:T(2,128)S(1)} %copy-done.2) | data formatting | bytes 2097152 | tf_op jit(solution)/shard_map/reshape | solution.py:460
  19.8 0.0 copy-done
  19.9 0.0 copy-start.5
  19.9 0.0 copy-start.6
  19.9 0.0 copy-start.9
  19.9 18.7 %shard_map.95.series = f32[16,256]{1,0:T(8,128)} custom-call(bf16[2,129,16,1024]{3,2,1,0:T(8,128)(2,1)} %kernel.3, f32[256,1024]{1,0:T(8,128)} %reshape.44.param, f32[3,176,256]{2,1,0:T(8,128)} %copy.18.fields, f32[3,2,176,256]{3,2,1,0:T(8,128)} %copy-done.1), custom_call_target="tpu_custom_call" | custom-call | tf_op jit(solution)/shard_map/pallas_call | solution.py:390
  38.6 0.0 copy-done.5
  38.6 0.6 copy.26
  39.2 0.0 copy-done.6
  39.2 0.6 copy.27
  39.8 0.0 copy-done.9
  39.8 0.7 broadcast_in_dim.20.noise
  40.5 9.8 %shard_map.96.weighted = f32[16,256]{1,0:T(8,128)} custom-call(f32[16,256]{1,0:T(8,128)} %shard_map.95.series, f32[16,256]{1,0:T(8,128)} %bitcast.21, f32[16,256]{1,0:T(8,128)} %broadcast_in_dim.20.noise, s32[16,256]{1,0:T(8,128)} %bitcast.20), custom_call_target="tpu_custom_call" | custom-call | tf_op jit(solution)/shard_map/pallas_call | solution.py:79
  50.3 10.6 %shard_map.97.part = bf16[32,8,1024]{2,1,0:T(8,128)(2,1)} custom-call(bf16[2,129,16,1024]{3,2,1,0:T(8,128)(2,1)} %kernel.3, f32[16,256]{1,0:T(8,128)} %shard_map.96.weighted, f32[3,256,176]{2,1,0:T(8,128)} %bitcast.19, f32[3,2,176,256]{3,2,1,0:T(8,128)} %copy-done.1), custom_call_target="tpu_custom_call" | custom-call | tf_op jit(solution)/shard_map/pallas_call | solution.py:438
  60.9 0.0 copy-start.4
  60.9 0.0 copy-start.7
  60.9 0.0 copy-start.8
  60.9 1.7 %reshape_reshape.3.param = f32[32,8,1024]{2,1,0:T(8,128)} reshape(f32[128,2,1024]{2,1,0:T(2,128)S(1)} %copy-done.2) | data formatting | bytes 2097152 | tf_op jit(solution)/shard_map/reshape;reshape | solution.py:472
  62.6 0.0 copy-done.4
  62.6 0.0 copy-done.7
  62.6 0.6 pad_maximum_fusion.3.coef
  63.3 0.0 copy-done.8
  63.3 0.7 copy.19.near
  63.9 42.5 %shard_map.98 = (f32[32,8,1024]{2,1,0:T(8,128)}, f32[32,8,1024]{2,1,0:T(8,128)}) custom-call(bf16[32,8,1024]{2,1,0:T(8,128)(2,1)} %shard_map.97.part, f32[32,8,1024]{2,1,0:T(8,128)} %reshape_reshape.3.param, f32[2,1024]{1,0:T(2,128)} %pad_maximum_fusion.3.coef, s32[8,4]{1,0:T(8,128)} %copy.19.near), custom_call_target="tpu_custom_call" | custom-call | tf_op jit(solution)/shard_map/pallas_call | solution.py:307
  106.4 0.0 copy-start.3
  106.4 2.9 %reshape.48 = f32[128,2,1024]{2,1,0:T(2,128)} reshape(f32[32,8,1024]{2,1,0:T(8,128)} %get-tuple-element.4) | data formatting | bytes 2097152 | tf_op jit(solution)/shard_map/reshape | solution.py:473
  109.3 0.0 copy-done.3
  109.3 1.6 %reshape.49 = f32[128,2,1024]{2,1,0:T(2,128)} reshape(f32[32,8,1024]{2,1,0:T(8,128)S(1)} %copy-done.3) | data formatting | bytes 2097152 | tf_op jit(solution)/shard_map/reshape | solution.py:473
  (14 shorter events, 0.2 us)
Async XLA Ops:
  15.2 2.3 %copy-start.1 = (f32[3,2,176,256]{3,2,1,0:T(8,128)}, f32[3,2,176,256]{3,2,1,0:T(8,128)S(1)}, u32[]{:S(2)}) copy-start(f32[3,2,176,256]{3,2,1,0:T(8,128)S(1)} %constant_dynamic-update-slice_fusion.sensors) | copy-start | bytes 3244036
  16.4 3.4 %copy-start = (f32[3,176,256]{1,2,0:T(8,128)}, f32[3,176,256]{1,2,0:T(8,128)S(1)}, u32[]{:S(2)}) copy-start(f32[3,176,256]{1,2,0:T(8,128)S(1)} %reshape.46) | copy-start | bytes 1622020
  16.5 1.7 %copy-start.2 = (f32[128,2,1024]{2,1,0:T(2,128)S(1)}, f32[128,2,1024]{2,1,0:T(2,128)}, u32[]{:S(2)}) copy-start(f32[128,2,1024]{2,1,0:T(2,128)} %param.9) | copy-start | bytes 3145732
  19.9 18.7 %copy-start.5 = (s32[16,128]{1,0:T(8,128)S(1)}, s32[16,128]{1,0:T(8,128)}, u32[]{:S(2)}) copy-start(s32[16,128]{1,0:T(8,128)} %param.12) | copy-start | bytes 24580
  19.9 19.3 %copy-start.6 = (f32[16,128]{1,0:T(8,128)S(1)}, f32[16,128]{1,0:T(8,128)}, u32[]{:S(2)}) copy-start(f32[16,128]{1,0:T(8,128)} %param.10) | copy-start | bytes 24580
  19.9 19.9 %copy-start.9 = (f32[16]{0:T(128)S(1)}, f32[16]{0:T(128)}, u32[]{:S(2)}) copy-start(f32[16]{0:T(128)} %param.11) | copy-start | bytes 196
  60.9 1.7 %copy-start.4 = (f32[1024]{0:T(1024)S(1)}, f32[1024]{0:T(1024)}, u32[]{:S(2)}) copy-start(f32[1024]{0:T(1024)} %param.14) | copy-start | bytes 12292
  60.9 1.7 %copy-start.7 = (f32[1024]{0:T(1024)S(1)}, f32[1024]{0:T(1024)}, u32[]{:S(2)}) copy-start(f32[1024]{0:T(1024)} %param.13) | copy-start | bytes 12292
  60.9 2.3 %copy-start.8 = (s32[8,4]{0,1:T(4,128)S(1)}, s32[8,4]{0,1:T(4,128)}, u32[]{:S(2)}) copy-start(s32[8,4]{0,1:T(4,128)} %param.15) | copy-start | bytes 388
  106.4 2.9 %copy-start.3 = (f32[32,8,1024]{2,1,0:T(8,128)S(1)}, f32[32,8,1024]{2,1,0:T(8,128)}, u32[]{:S(2)}) copy-start(f32[32,8,1024]{2,1,0:T(8,128)} %get-tuple-element.5) | copy-start | bytes 3145732

commit v3 on v2

--- a/solution.py
+++ b/solution.py
@@ -2,6 +2,7 @@
 
 import jax
 import jax.numpy as jnp
+import numpy as np
 from jax import lax
 from jax.experimental import pallas as pl
 from jax.experimental.pallas import tpu as pltpu
@@ -17,18 +18,13 @@
 
 def tables(length):
     period = 2 * length
-    frequency = jnp.arange(length + 1, dtype=jnp.int32)
-    moment = jnp.arange(length, dtype=jnp.int32)
-    phases = frequency[:, None] * moment[None, :] % period
-    angles = phases.astype(jnp.float32) * (2.0 * jnp.pi / period)
-    cosine = jnp.cos(angles)
-    sines = jnp.sin(angles)
-    forward = jnp.concatenate([cosine, -sines], 0)
-    weight = (
-        jnp.where((frequency == 0) | (frequency == length), 1.0, 2.0).astype(jnp.float32) / period
-    )
-    backward = jnp.concatenate([weight[:, None] * cosine, -weight[:, None] * sines], 0)
-    return (forward, backward)
+    frequency = np.arange(length + 1)
+    phases = frequency[:, None] * np.arange(length)[None, :] % period
+    angles = phases * (2.0 * np.pi / period)
+    cosine, sines = np.cos(angles), np.sin(angles)
+    forward = np.stack([cosine, -sines], 0)
+    weight = np.where((frequency == 0) | (frequency == length), 1.0, 2.0) / period
+    return forward, forward * weight[:, None]
 
 
 MESH = pl.DeviceIdType.MESH
@@ -63,10 +59,15 @@
     for step, copy in enumerate(copies):
         copy.wait_recv()
         total = total + landed[step]
-    deviation = noise[...]
-    scaled = (total - observed[...]) / deviation
+    samples = series.shape[1] // observed.shape[1]
+
+    def widen(ref):
+        return jnp.concatenate([ref[...]] * samples, 1)
+
+    deviation = widen(noise)
+    scaled = (total - widen(observed)) / deviation
     robust = jnp.where(
-        flags[...] == 1, jnp.clip(scaled, -huber_limit, huber_limit), scaled
+        widen(flags) == 1, jnp.clip(scaled, -huber_limit, huber_limit), scaled
     )
     weighted[...] = robust / deviation
     for copy in copies:
@@ -117,7 +118,7 @@
 
 def field_kernel(
     groups, tiles, part, param, coef, near, grad_out, dir_out,
-    landed, outgoing, misfit, field, coefs, grad, link, inverse, direction, grad_send, dir_send,
+    landed, outgoing, misfit, field, coefs, grad, link, inverse, even, odd, grad_send, dir_send,
     gathered, a_send, a_recv, p_send, p_recv, c_send, c_recv, b_send, b_recv, g_send, g_recv,
     e_send, e_recv,
 ):
@@ -209,7 +210,7 @@
         total = grad[tile] + misfit[tile]
         grad[tile] = total
         grad_send[tile] = total.astype(jnp.bfloat16)
-        direction[0, tile] = total * inverse[tile]
+        even[tile] = total * inverse[tile]
         return carry
 
     lax.fori_loop(0, tiles, add_misfit, 0)
@@ -247,30 +248,33 @@
                 onward.append(copy)
         return onward
 
-    def sweep(count, carry):
-        old, new = lax.rem(count, 2), lax.rem(count + 1, 2)
-
-        def relax(tile, inner):
+    def sweep(count):
+        old, new = (even, odd) if count % 2 == 0 else (odd, even)
+
+        def relax(tile, carry):
             sums = grid_sum(
-                lambda i, j: direction[old, i, :, j * LANES : (j + 1) * LANES],
-                tile, near, rows, chunks,
+                lambda i, j: old[i, :, j * LANES : (j + 1) * LANES], tile, near, rows, chunks
             )
             for j, total in enumerate(sums):
                 at = slice(j * LANES, (j + 1) * LANES)
-                direction[new, tile, :, at] = (
-                    grad[tile, :, at] + link[tile, :, at] * total
-                ) * inverse[tile, :, at]
-            return inner
-
-        return lax.fori_loop(0, tiles, relax, carry)
+                new[tile, :, at] = (grad[tile, :, at] + link[tile, :, at] * total) * inverse[
+                    tile, :, at
+                ]
+            return carry
+
+        lax.fori_loop(0, tiles, relax, 0, unroll=4)
 
     g_copies = exchange(0, grad_send)
-    lax.fori_loop(0, 3, sweep, 0)
+    for count in range(3):
+        sweep(count)
     g_onward = forward_on(0, g_copies)
-    lax.fori_loop(3, SWEEPS - 1, sweep, 0)
+    for count in range(3, SWEEPS - 1):
+        sweep(count)
+
+    last = odd if SWEEPS % 2 == 0 else even
 
     def pack(tile, carry):
-        dir_send[tile] = direction[(SWEEPS - 1) % 2, tile].astype(jnp.bfloat16)
+        dir_send[tile] = last[tile].astype(jnp.bfloat16)
         return carry
 
     lax.fori_loop(0, tiles, pack, 0)
@@ -318,7 +322,8 @@
             pltpu.VMEM(block, f32),
             pltpu.VMEM(block, f32),
             pltpu.VMEM(block, f32),
-            pltpu.VMEM((2,) + block, f32),
+            pltpu.VMEM(block, f32),
+            pltpu.VMEM(block, f32),
             pltpu.VMEM(block, bf16),
             pltpu.VMEM(block, bf16),
             pltpu.VMEM((2, groups) + block, bf16),
@@ -328,8 +333,27 @@
     )(part, param, coef, neighbours)
 
 
-HIGH = lax.Precision.HIGHEST
 LAST = (((1,), (1,)), ((), ()))
+PLAIN = (((1,), (0,)), ((), ()))
+
+
+def split(values):
+    high = values.astype(jnp.bfloat16)
+    return high, (values - high.astype(jnp.float32)).astype(jnp.bfloat16)
+
+
+def halves(table):
+    high = table.astype(np.float32).astype(jnp.bfloat16)
+    low = (table - high.astype(np.float64)).astype(np.float32).astype(jnp.bfloat16)
+    return np.stack([high, low], 1)
+
+
+def dot3(left, right, dims=PLAIN):
+    parts = [(left[0], right[0]), (left[0], right[1]), (left[1], right[0])]
+    high, *low = [
+        lax.dot_general(a, b, dims, preferred_element_type=jnp.float32) for a, b in parts
+    ]
+    return high + (low[0] + low[1])
 
 
 def block_tables(length, samples):
@@ -338,33 +362,44 @@
     size = max(d for d in range(1, 65) if count % d == 0)
     padded = -(-size // 4) * 4
     blocks = count // size
-    eye = jnp.eye(samples, dtype=jnp.float32)
+    eye = np.eye(samples)
 
     def arrange(table):
         table = table.reshape(2, blocks, size, length)
-        return jnp.pad(table, ((0, 0), (0, 0), (0, padded - size), (0, 0)))
+        return np.pad(table, ((0, 0), (0, 0), (0, padded - size), (0, 0)))
 
     fore, back = arrange(forward), arrange(backward)
-    turned = jnp.stack([back[1], -back[0]], 0)
+    turned = np.stack([back[1], -back[0]], 0)
     rows = samples * 2 * padded
-    fields = jnp.einsum("jkft,bd->kbjftd", fore, eye).reshape(blocks, rows, -1)
+    fields = np.einsum("jkft,bd->kbjftd", fore, eye).reshape(blocks, rows, -1)
     sensors = [
-        jnp.einsum("jkft,bd->kbjfdt", table, eye).reshape(blocks, rows, -1)
+        np.einsum("jkft,bd->kbjfdt", table, eye).reshape(blocks, rows, -1)
         for table in (back, turned)
     ]
-    return fields, jnp.stack(sensors, 1), size, padded
-
-
-def diagonal(shape, width, padded, frequency_dim):
-    own = lax.broadcasted_iota(jnp.int32, shape, frequency_dim)
-    other = lax.broadcasted_iota(jnp.int32, shape, 1 - frequency_dim)
-    return own // width == lax.rem(other, padded)
-
-
-def predict_kernel(padded, kernel, param, fields, sensors, series):
+    return (
+        halves(fields),
+        halves(fields.transpose(0, 2, 1)),
+        np.stack([halves(table) for table in sensors], 1),
+        size,
+        padded,
+    )
+
+
+def predict_kernel(padded, kernel, param, fields, sensors, series, high, low):
     size, sensor_count, cells = kernel.shape[1:]
-    spectrum = jnp.dot(fields[0], param[...], precision=HIGH, preferred_element_type=jnp.float32)
-    spectrum = spectrum.astype(jnp.bfloat16)
+
+    @pl.when(pl.program_id(0) == 0)
+    def _():
+        series[...] = jnp.zeros_like(series)
+        first, second = split(param[...].reshape(high.shape))
+        high[...] = first
+        low[...] = second
+
+    spectrum = dot3((fields[0, 0], fields[0, 1]), (high[...], low[...])).astype(jnp.bfloat16)
+    columns = spectrum.shape[0]
+    other = lax.rem(lax.broadcasted_iota(jnp.int32, (1, 1, columns), 2), padded)
+    own = lax.broadcasted_iota(jnp.int32, (size, 1, columns), 0)
+    keep = own == other
     total = jnp.zeros(series.shape, jnp.float32)
     for i in range(2):
         product = lax.dot_general(
@@ -372,20 +407,14 @@
             spectrum,
             LAST,
             preferred_element_type=jnp.float32,
-        )
-        product = jnp.where(diagonal(product.shape, sensor_count, padded, 0), product, 0.0)
-        timed = jnp.dot(product, sensors[0, i], precision=HIGH, preferred_element_type=jnp.float32)
-        total = total + jnp.sum(timed.reshape(size, sensor_count, -1), 0)
-
-    @pl.when(pl.program_id(0) == 0)
-    def _():
-        series[...] = jnp.zeros_like(series)
-
+        ).reshape(size, sensor_count, columns)
+        picked = jnp.sum(jnp.where(keep, product, 0.0), 0)
+        total = total + dot3(split(picked), (sensors[0, i, 0], sensors[0, i, 1]))
     series[...] += total
 
 
 def predict(kernel, param, fields, sensors, size, padded):
-    blocks, rows, width = fields.shape
+    blocks, _, rows, width = fields.shape
     sensor_count, cells = kernel.shape[2:]
     return pl.pallas_call(
         functools.partial(predict_kernel, padded),
@@ -393,33 +422,34 @@
         grid=(blocks,),
         in_specs=[
             pl.BlockSpec((2, size, sensor_count, cells), lambda k: (0, k, 0, 0)),
-            pl.BlockSpec(param.shape, lambda k: (0, 0)),
-            pl.BlockSpec((1, rows, width), lambda k: (k, 0, 0)),
+            pl.BlockSpec(param.shape, lambda k: (0, 0, 0)),
             pl.BlockSpec((1, 2, rows, width), lambda k: (k, 0, 0, 0)),
+            pl.BlockSpec((1, 2, 2, rows, width), lambda k: (k, 0, 0, 0, 0)),
         ],
         out_specs=pl.BlockSpec((sensor_count, width), lambda k: (0, 0)),
+        scratch_shapes=[pltpu.VMEM((width, cells), jnp.bfloat16)] * 2,
     )(kernel, param, fields, sensors)
 
 
 def backward_kernel(padded, blocks, kernel, weighted, fields, sensors, part, total):
     size, sensor_count, cells = kernel.shape[1:]
-    rows = sensors.shape[2]
+    rows = sensors.shape[3]
     pairs = size * sensor_count
-    copies = lax.rem(lax.broadcasted_iota(jnp.int32, (sensor_count, pairs), 1), sensor_count)
+    copies = lax.rem(lax.broadcasted_iota(jnp.int32, (1, pairs), 1), sensor_count)
     copies = copies == lax.broadcasted_iota(jnp.int32, (sensor_count, pairs), 0)
     copies = jnp.where(copies, 1.0, 0.0).astype(jnp.bfloat16)
-    keep = diagonal((rows, pairs), sensor_count, padded, 1)
+    column = lax.broadcasted_iota(jnp.int32, (1, pairs), 1) // sensor_count
+    keep = column == lax.rem(lax.broadcasted_iota(jnp.int32, (rows, 1), 0), padded)
+    source = split(weighted[...])
     back = jnp.zeros((rows, cells), jnp.float32)
     for i in range(2):
-        adjoint = lax.dot_general(
-            sensors[0, i], weighted[...], LAST, precision=HIGH, preferred_element_type=jnp.float32
-        )
+        adjoint = dot3((sensors[0, i, 0], sensors[0, i, 1]), source, LAST)
         wide = jnp.dot(adjoint.astype(jnp.bfloat16), copies, preferred_element_type=jnp.float32)
         wide = jnp.where(keep, wide, 0.0).astype(jnp.bfloat16)
         back = back + jnp.dot(
             wide, kernel[i].reshape(pairs, cells), preferred_element_type=jnp.float32
         )
-    misfit = jnp.dot(fields[0], back, precision=HIGH, preferred_element_type=jnp.float32)
+    misfit = dot3((fields[0, 0], fields[0, 1]), split(back))
 
     @pl.when(pl.program_id(0) == 0)
     def _():
@@ -433,7 +463,7 @@
 
 
 def back_project(kernel, weighted, fields, sensors, size, padded, shape):
-    blocks, width, rows = fields.shape
+    blocks, _, width, rows = fields.shape
     sensor_count, cells = kernel.shape[2:]
     return pl.pallas_call(
         functools.partial(backward_kernel, padded, blocks),
@@ -442,8 +472,8 @@
         in_specs=[
             pl.BlockSpec((2, size, sensor_count, cells), lambda k: (0, k, 0, 0)),
             pl.BlockSpec(weighted.shape, lambda k: (0, 0)),
-            pl.BlockSpec((1, width, rows), lambda k: (k, 0, 0)),
-            pl.BlockSpec((1, 2, rows, weighted.shape[1]), lambda k: (k, 0, 0, 0)),
+            pl.BlockSpec((1, 2, width, rows), lambda k: (k, 0, 0, 0)),
+            pl.BlockSpec((1, 2, 2, rows, weighted.shape[1]), lambda k: (k, 0, 0, 0, 0)),
         ],
         out_specs=pl.BlockSpec(shape, lambda k: (0, 0, 0)),
         scratch_shapes=[pltpu.VMEM((width, cells), jnp.float32)],
@@ -454,22 +484,22 @@
     kernel, param, observed, noise_scale, robust_flags, kappa_field, coupling, neighbours
 ):
     length, samples, cell_count = param.shape
-    fields, sensors, size, padded = block_tables(length, samples)
+    fields, turned, sensors, size, padded = block_tables(length, samples)
     devices = lax.axis_size("sens") * lax.axis_size("par")
     blocks = (devices, length * samples // devices, cell_count)
-    flat = param.reshape(length * samples, cell_count)
+    flat = param.reshape(blocks)
     series = predict(kernel, flat, fields, sensors, size, padded)
     weighted = residual(
         series,
-        jnp.tile(observed, (1, samples)),
+        observed,
         noise_scale,
-        jnp.tile(robust_flags, (1, samples)),
+        robust_flags,
     )
     part = back_project(
-        kernel, weighted, fields.transpose(0, 2, 1), sensors, size, padded, blocks
+        kernel, weighted, turned, sensors, size, padded, blocks
     )
     coef = jnp.stack([coupling, kappa_field + 4.0 * coupling], 0)
-    gradient, direction = field_stage(part, flat.reshape(blocks), coef, neighbours)
+    gradient, direction = field_stage(part, flat, coef, neighbours)
     return gradient.reshape(param.shape), direction.reshape(param.shape)
 
 

time: 111 us -> 83.5 us (0.75)
  Pallas kernels: 81.6 us -> 69.2 us
  local copies, waits for them, and re-layouts: 23.2 us -> 11.2 us
  other arithmetic: 5.29 us -> 2 us
    pallas_call x1, Pallas kernels: 18.7 us -> 9.86 us  [predict(): pl.pallas_call(functools.partial(predict_kernel, padded), out_shape=jax.S...]
    transpose x2 -> x0, local copies, waits for them, and re-layouts: 5.05 us -> none  [block_tables(): jnp.einsum('jkft,bd->kbjfdt', table, eye).reshape(blocks, rows, -1)]
    another operation x7 -> x0, local copies, waits for them, and re-layouts: 4.92 us -> none  [the longest x3 3 us: block_tables(): return (fields, jnp.stack(sensors, 1), size, padded)]
    transpose x1 -> x0, other arithmetic: 4.02 us -> none  [block_tables(): jnp.einsum('jkft,bd->kbjfdt', table, eye).reshape(blocks, rows, -1)]
    pallas_call x1, Pallas kernels: 10.6 us -> 8.74 us  [back_project(): pl.pallas_call(functools.partial(backward_kernel, padded, blocks), out_sh...]
    unnamed x26 -> x1, local copies, waits for them, and re-layouts: 3.02 us -> 1.35 us
    pallas_call x1, Pallas kernels: 42.5 us -> 40.8 us  [field_stage(): pl.pallas_call(functools.partial(field_kernel, groups, tiles), out_shape=...]
    reshape x2, local copies, waits for them, and re-layouts: 4.49 us -> 5.62 us  [per_device(): return (gradient.reshape(param.shape), direction.reshape(param.shape))]
where the time goes in v3:
time: 83.5 us; the launch traced here: 83.1 us
  Pallas kernels  69.2 us (83%)
  local copies, waits for them, and re-layouts  11.2 us (13%)
  other arithmetic  2 us (2%)
    pallas_call x1, Pallas kernels, field_stage(): pl.pallas_call(functools.partial(field_kernel, groups, tiles), out_shape=...  40.8 us
    pallas_call x1, Pallas kernels, predict(): pl.pallas_call(functools.partial(predict_kernel, padded), out_shape=jax.S...  9.86 us
    pallas_call x1, Pallas kernels, residual(): pl.pallas_call(functools.partial(residual_kernel, tiles), out_shape=jax.S...  9.79 us
    pallas_call x1, Pallas kernels, back_project(): pl.pallas_call(functools.partial(backward_kernel, padded, blocks), out_sh...  8.74 us
    reshape x2, local copies, waits for them, and re-layouts, per_device(): return (gradient.reshape(param.shape), direction.reshape(param.shape))  5.62 us
    reshape x1, local copies, waits for them, and re-layouts, per_device(): flat = param.reshape(blocks)  2.91 us

profile of v3, /device:TPU:0, one launch (start us, length us, event | category | flops | bytes accessed | tf_op | source)
XLA Modules:
  0.0 83.1 jit_solution(7792081591685646508)
XLA Ops:
  0.6 0.7 multiply_add_fusion
  1.3 1.3 %pad_maximum_fusion.coef = f32[2,1024]{1,0:T(2,128)} fusion(f32[1,1024]{1,0:T(1,128)S(1)} %bitcast.3, f32[1,1024]{1,0:T(1,128)} %bitcast.2), kind=kLoop, calls=%fused_computation | loop fusion | flops 2048 | bytes 16384 | tf_op jit(solution)/shard_map/stack | solution.py:501
  2.6 1.3 %copy.13.near = s32[8,4]{1,0:T(8,128)} copy(s32[8,4]{0,1:T(4,128)} %param.18) | data formatting | bytes 256 | tf_op args[7]
  4.0 1.3 %broadcast_in_dim.2.noise = f32[16,128]{1,0:T(8,128)} broadcast(f32[16]{0:T(128)} %param.14), dimensions={0} | broadcast | bytes 8256 | tf_op jit(solution)/shard_map/broadcast_in_dim | solution.py:79
  5.3 2.9 %reshape.14.param = f32[32,8,1024]{2,1,0:T(8,128)} reshape(f32[128,2,1024]{2,1,0:T(2,128)} %param.12) | data formatting | bytes 2097152 | tf_op jit(solution)/shard_map/reshape | solution.py:490
  8.2 9.9 %shard_map.122.series = f32[16,256]{1,0:T(8,128)} custom-call(bf16[2,129,16,1024]{3,2,1,0:T(8,128)(2,1)} %kernel.3, f32[32,8,1024]{2,1,0:T(8,128)} %reshape.14.param, bf16[3,2,176,256]{3,2,1,0:T(8,128)(2,1)} %constant.8.clone.fields, bf16[3,2,2,176,256]{4,3,2,1,0:T(8,128)(2,1)} %constant.9.clone.sensors), custom_call_target="tpu_custom_call" | custom-call | tf_op jit(solution)/shard_map/pallas_call | solution.py:419
  18.1 9.8 %shard_map.123.weighted = f32[16,256]{1,0:T(8,128)} custom-call(f32[16,256]{1,0:T(8,128)} %shard_map.122.series, f32[16,128]{1,0:T(8,128)} %observed.1, f32[16,128]{1,0:T(8,128)} %broadcast_in_dim.2.noise, s32[16,128]{1,0:T(8,128)} %flags.1), custom_call_target="tpu_custom_call" | custom-call | tf_op jit(solution)/shard_map/pallas_call | solution.py:80
  27.9 8.7 %shard_map.124.part = bf16[32,8,1024]{2,1,0:T(8,128)(2,1)} custom-call(bf16[2,129,16,1024]{3,2,1,0:T(8,128)(2,1)} %kernel.3, f32[16,256]{1,0:T(8,128)} %shard_map.123.weighted, bf16[3,2,256,176]{3,2,1,0:T(8,128)(2,1)} %constant.10.clone.fields, bf16[3,2,2,176,256]{4,3,2,1,0:T(8,128)(2,1)} %constant.9.clone.sensors), custom_call_target="tpu_custom_call" | custom-call | tf_op jit(solution)/shard_map/pallas_call | solution.py:468
  36.6 40.8 %shard_map.125 = (f32[32,8,1024]{2,1,0:T(8,128)}, f32[32,8,1024]{2,1,0:T(8,128)}) custom-call(bf16[32,8,1024]{2,1,0:T(8,128)(2,1)} %shard_map.124.part, f32[32,8,1024]{2,1,0:T(8,128)} %reshape.14.param, f32[2,1024]{1,0:T(2,128)} %pad_maximum_fusion.coef, s32[8,4]{1,0:T(8,128)} %copy.13.near), custom_call_target="tpu_custom_call" | custom-call | tf_op jit(solution)/shard_map/pallas_call | solution.py:311
  77.4 2.8 %reshape.15 = f32[128,2,1024]{2,1,0:T(2,128)} reshape(f32[32,8,1024]{2,1,0:T(8,128)} %get-tuple-element.4) | data formatting | bytes 2097152 | tf_op jit(solution)/shard_map/reshape | solution.py:503
  80.3 2.8 %reshape.16 = f32[128,2,1024]{2,1,0:T(2,128)} reshape(f32[32,8,1024]{2,1,0:T(8,128)} %get-tuple-element.5) | data formatting | bytes 2097152 | tf_op jit(solution)/shard_map/reshape | solution.py:503

commit v4 on v3

--- a/solution.py
+++ b/solution.py
@@ -128,6 +128,11 @@
     group_at = [lax.rem(sens + k, groups) for k in range(groups)]
     tile_at = [lax.rem(par + q, tiles) for q in range(tiles)]
     source_at = [lax.rem(par + tiles - q, tiles) for q in range(tiles)]
+    beside = [
+        sens + 1 - 2 * lax.rem(sens, 2),
+        sens + 2 - 4 * lax.rem(sens // 2, 2),
+    ]
+    targets = beside if groups == 4 else group_at[1:]
 
     barrier = pltpu.get_barrier_semaphore()
     for k in range(1, groups):
@@ -236,17 +241,32 @@
             if q:
                 copies[q - 1].wait_recv()
             piece = gathered.at[which, sens, source_at[q]]
-            for k in range(1, groups):
+            for k, target in enumerate(targets):
                 copy = remote(
                     piece,
                     piece,
-                    e_send.at[which, k - 1, q],
-                    e_recv.at[which, k - 1, q],
-                    (group_at[k], par),
+                    e_send.at[which, k, q],
+                    e_recv.at[which, k, q],
+                    (target, par),
                 )
                 copy.start()
                 onward.append(copy)
         return onward
+
+    def relay(which, onward):
+        if groups != 4:
+            return onward, []
+        second = []
+        for q in range(tiles):
+            via = q % 2
+            onward[2 * q + via].wait_recv()
+            piece = gathered.at[which, beside[via], source_at[q]]
+            copy = remote(
+                piece, piece, e_send.at[which, 2, q], e_recv.at[which, 2, q], (beside[1 - via], par)
+            )
+            copy.start()
+            second.append(copy)
+        return [onward[2 * q + 1 - q % 2] for q in range(tiles)] + second, second
 
     def sweep(count):
         old, new = (even, odd) if count % 2 == 0 else (odd, even)
@@ -265,12 +285,10 @@
         lax.fori_loop(0, tiles, relax, 0, unroll=4)
 
     g_copies = exchange(0, grad_send)
-    for count in range(3):
+    sweep(0)
+    g_onward = forward_on(0, g_copies)
+    for count in range(1, SWEEPS - 1):
         sweep(count)
-    g_onward = forward_on(0, g_copies)
-    for count in range(3, SWEEPS - 1):
-        sweep(count)
-
     last = odd if SWEEPS % 2 == 0 else even
 
     def pack(tile, carry):
@@ -279,7 +297,9 @@
 
     lax.fori_loop(0, tiles, pack, 0)
     d_copies = exchange(1, dir_send)
+    g_waits, g_second = relay(0, g_onward)
     d_onward = forward_on(1, d_copies)
+    d_waits, d_second = relay(1, d_onward)
 
     def unpack(which, out):
         def one(index, carry):
@@ -289,13 +309,14 @@
 
         lax.fori_loop(0, groups * tiles, one, 0)
 
-    for copy in g_onward:
+    for copy in g_waits:
         copy.wait_recv()
     unpack(0, grad_out)
-    for copy in d_onward:
+    for copy in d_waits:
         copy.wait_recv()
     unpack(1, dir_out)
-    for copy in list(a_copies.values()) + p_copies + b_copies + g_copies + d_copies + g_onward + d_onward:
+    started = list(a_copies.values()) + p_copies + b_copies + g_copies + d_copies
+    for copy in started + g_onward + d_onward + g_second + d_second:
         copy.wait_send()
 
 

time: 83.5 us -> 85.4 us (1.023)
  Pallas kernels: 69.2 us -> 71.2 us
    pallas_call x1, Pallas kernels: 40.8 us -> 42.8 us  [field_stage(): pl.pallas_call(functools.partial(field_kernel, groups, tiles), out_shape=...]
where the time goes in v4:
time: 85.4 us; the launch traced here: 85 us
  Pallas kernels  71.2 us (83%)
  local copies, waits for them, and re-layouts  11.2 us (13%)
  other arithmetic  2 us (2%)
    pallas_call x1, Pallas kernels, field_stage(): pl.pallas_call(functools.partial(field_kernel, groups, tiles), out_shape=...  42.8 us
    pallas_call x1, Pallas kernels, predict(): pl.pallas_call(functools.partial(predict_kernel, padded), out_shape=jax.S...  9.86 us
    pallas_call x1, Pallas kernels, residual(): pl.pallas_call(functools.partial(residual_kernel, tiles), out_shape=jax.S...  9.79 us
    pallas_call x1, Pallas kernels, back_project(): pl.pallas_call(functools.partial(backward_kernel, padded, blocks), out_sh...  8.74 us
    reshape x2, local copies, waits for them, and re-layouts, per_device(): return (gradient.reshape(param.shape), direction.reshape(param.shape))  5.62 us
    reshape x1, local copies, waits for them, and re-layouts, per_device(): flat = param.reshape(blocks)  2.91 us

profile of v4, /device:TPU:0, one launch (start us, length us, event | category | flops | bytes accessed | tf_op | source)
XLA Modules:
  0.0 85.0 jit_solution(11389901146358819924)
XLA Ops:
  0.6 0.7 multiply_add_fusion
  1.3 1.3 %pad_maximum_fusion.coef = f32[2,1024]{1,0:T(2,128)} fusion(f32[1,1024]{1,0:T(1,128)S(1)} %bitcast.3, f32[1,1024]{1,0:T(1,128)} %bitcast.2), kind=kLoop, calls=%fused_computation | loop fusion | flops 2048 | bytes 16384 | tf_op jit(solution)/shard_map/stack | solution.py:522
  2.6 1.3 %copy.13.near = s32[8,4]{1,0:T(8,128)} copy(s32[8,4]{0,1:T(4,128)} %param.18) | data formatting | bytes 256 | tf_op args[7]
  4.0 1.3 %broadcast_in_dim.2.noise = f32[16,128]{1,0:T(8,128)} broadcast(f32[16]{0:T(128)} %param.14), dimensions={0} | broadcast | bytes 8256 | tf_op jit(solution)/shard_map/broadcast_in_dim | solution.py:79
  5.3 2.9 %reshape.14.param = f32[32,8,1024]{2,1,0:T(8,128)} reshape(f32[128,2,1024]{2,1,0:T(2,128)} %param.12) | data formatting | bytes 2097152 | tf_op jit(solution)/shard_map/reshape | solution.py:511
  8.2 9.9 %shard_map.122.series = f32[16,256]{1,0:T(8,128)} custom-call(bf16[2,129,16,1024]{3,2,1,0:T(8,128)(2,1)} %kernel.3, f32[32,8,1024]{2,1,0:T(8,128)} %reshape.14.param, bf16[3,2,176,256]{3,2,1,0:T(8,128)(2,1)} %constant.8.clone.fields, bf16[3,2,2,176,256]{4,3,2,1,0:T(8,128)(2,1)} %constant.9.clone.sensors), custom_call_target="tpu_custom_call" | custom-call | tf_op jit(solution)/shard_map/pallas_call | solution.py:440
  18.1 9.8 %shard_map.123.weighted = f32[16,256]{1,0:T(8,128)} custom-call(f32[16,256]{1,0:T(8,128)} %shard_map.122.series, f32[16,128]{1,0:T(8,128)} %observed.1, f32[16,128]{1,0:T(8,128)} %broadcast_in_dim.2.noise, s32[16,128]{1,0:T(8,128)} %flags.1), custom_call_target="tpu_custom_call" | custom-call | tf_op jit(solution)/shard_map/pallas_call | solution.py:80
  27.9 8.7 %shard_map.124.part = bf16[32,8,1024]{2,1,0:T(8,128)(2,1)} custom-call(bf16[2,129,16,1024]{3,2,1,0:T(8,128)(2,1)} %kernel.3, f32[16,256]{1,0:T(8,128)} %shard_map.123.weighted, bf16[3,2,256,176]{3,2,1,0:T(8,128)(2,1)} %constant.10.clone.fields, bf16[3,2,2,176,256]{4,3,2,1,0:T(8,128)(2,1)} %constant.9.clone.sensors), custom_call_target="tpu_custom_call" | custom-call | tf_op jit(solution)/shard_map/pallas_call | solution.py:489
  36.6 42.8 %shard_map.125 = (f32[32,8,1024]{2,1,0:T(8,128)}, f32[32,8,1024]{2,1,0:T(8,128)}) custom-call(bf16[32,8,1024]{2,1,0:T(8,128)(2,1)} %shard_map.124.part, f32[32,8,1024]{2,1,0:T(8,128)} %reshape.14.param, f32[2,1024]{1,0:T(2,128)} %pad_maximum_fusion.coef, s32[8,4]{1,0:T(8,128)} %copy.13.near), custom_call_target="tpu_custom_call" | custom-call | tf_op jit(solution)/shard_map/pallas_call | solution.py:332
  79.4 2.8 %reshape.15 = f32[128,2,1024]{2,1,0:T(2,128)} reshape(f32[32,8,1024]{2,1,0:T(8,128)} %get-tuple-element.4) | data formatting | bytes 2097152 | tf_op jit(solution)/shard_map/reshape | solution.py:524
  82.2 2.8 %reshape.16 = f32[128,2,1024]{2,1,0:T(2,128)} reshape(f32[32,8,1024]{2,1,0:T(8,128)} %get-tuple-element.5) | data formatting | bytes 2097152 | tf_op jit(solution)/shard_map/reshape | solution.py:524

commit v5 on v3

--- a/solution.py
+++ b/solution.py
@@ -64,7 +64,11 @@
     def widen(ref):
         return jnp.concatenate([ref[...]] * samples, 1)
 
-    deviation = widen(noise)
+    count = noise.shape[1]
+    across = lax.broadcasted_iota(jnp.int32, (count, count), 1)
+    down = lax.broadcasted_iota(jnp.int32, (count, count), 0)
+    spread = jnp.where(across == down, jnp.broadcast_to(noise[...], (count, count)), 0.0)
+    deviation = jnp.sum(spread, 1, keepdims=True)
     scaled = (total - widen(observed)) / deviation
     robust = jnp.where(
         widen(flags) == 1, jnp.clip(scaled, -huber_limit, huber_limit), scaled
@@ -76,7 +80,6 @@
 
 def residual(series, observed, noise_scale, robust_flags):
     tiles = lax.axis_size("par")
-    spread = jnp.broadcast_to(noise_scale[:, None], observed.shape)
     return pl.pallas_call(
         functools.partial(residual_kernel, tiles),
         out_shape=jax.ShapeDtypeStruct(series.shape, jnp.float32),
@@ -88,13 +91,13 @@
             pltpu.SemaphoreType.DMA((tiles - 1,)),
         ],
         compiler_params=pltpu.CompilerParams(collective_id=0, has_side_effects=True),
-    )(series, observed, spread, robust_flags)
+    )(series, observed, noise_scale[None], robust_flags)
 
 
 def grid_sum(load, tile, near, rows, chunks):
     lane = lax.broadcasted_iota(jnp.int32, (rows, LANES), 1)
     column = lax.rem(lane, TSIDE)
-    beside = [near[tile, side] for side in range(4)]
+    beside = [near[side, tile] for side in range(4)]
     west, east, south, north = (jnp.maximum(index, 0) for index in beside)
     has_west, has_east, has_south, has_north = (
         jnp.minimum(index + 1, 1).astype(jnp.float32) for index in beside
@@ -117,8 +120,8 @@
 
 
 def field_kernel(
-    groups, tiles, part, param, coef, near, grad_out, dir_out,
-    landed, outgoing, misfit, field, coefs, grad, link, inverse, even, odd, grad_send, dir_send,
+    groups, tiles, part, param, kappa, coupling, near, grad_out, dir_out,
+    landed, outgoing, misfit, field, kappas, couplings, grad, link, inverse, even, odd, grad_send, dir_send,
     gathered, a_send, a_recv, p_send, p_recv, c_send, c_recv, b_send, b_recv, g_send, g_recv,
     e_send, e_recv,
 ):
@@ -152,7 +155,10 @@
     for q in range(1, tiles):
         device = (sens, tile_at[q])
         p_copies.append(
-            remote(coef, coefs.at[par], c_send.at[q - 1], c_recv.at[q - 1], device)
+            remote(kappa, kappas.at[par], c_send.at[0, q - 1], c_recv.at[0, q - 1], device)
+        )
+        p_copies.append(
+            remote(coupling, couplings.at[par], c_send.at[1, q - 1], c_recv.at[1, q - 1], device)
         )
         p_copies.append(
             remote(
@@ -166,7 +172,8 @@
     for copy in p_copies:
         copy.start()
     field[par] = param[sens * tiles + par]
-    coefs[par] = coef[...]
+    kappas[par] = kappa[...]
+    couplings[par] = coupling[...]
 
     b_copies = []
     for q in order:
@@ -191,8 +198,8 @@
         copy.wait_recv()
 
     def spread(tile, carry):
-        both = coefs[tile]
-        strength, diagonal = both[0:1], both[1:2]
+        strength = couplings[tile]
+        diagonal = kappas[tile] + 4.0 * strength
         link[tile] = jnp.broadcast_to(strength, (rows, cells))
         inverse[tile] = jnp.broadcast_to(1.0 / diagonal, (rows, cells))
         for j, total in enumerate(
@@ -299,7 +306,7 @@
         copy.wait_send()
 
 
-def field_stage(part, param, coef, neighbours):
+def field_stage(part, param, kappa, coupling, neighbours):
     groups, tiles = lax.axis_size("sens"), lax.axis_size("par")
     rows, cells = part.shape[1:]
     f32, bf16 = jnp.float32, jnp.bfloat16
@@ -307,18 +314,19 @@
     dma = pltpu.SemaphoreType.DMA
     block = (tiles, rows, cells)
     vmem, smem = pl.BlockSpec(memory_space=pltpu.VMEM), pl.BlockSpec(memory_space=pltpu.SMEM)
-    sems = [(groups - 1, tiles), (tiles - 1,), (tiles - 1,), (tiles - 1,), (2, tiles - 1), (2, groups - 1, tiles)]
+    sems = [(groups - 1, tiles), (tiles - 1,), (2, tiles - 1), (tiles - 1,), (2, tiles - 1), (2, groups - 1, tiles)]
     return pl.pallas_call(
         functools.partial(field_kernel, groups, tiles),
         out_shape=(full, full),
-        in_specs=[vmem, vmem, vmem, smem],
+        in_specs=[vmem, vmem, vmem, vmem, smem],
         out_specs=(vmem, vmem),
         scratch_shapes=[
             pltpu.VMEM((groups - 1,) + block, bf16),
             pltpu.VMEM((tiles - 1, rows, cells), f32),
             pltpu.VMEM(block, f32),
             pltpu.VMEM(block, f32),
-            pltpu.VMEM((tiles, 2, cells), f32),
+            pltpu.VMEM((tiles, 1, cells), f32),
+            pltpu.VMEM((tiles, 1, cells), f32),
             pltpu.VMEM(block, f32),
             pltpu.VMEM(block, f32),
             pltpu.VMEM(block, f32),
@@ -330,7 +338,7 @@
         ]
         + [dma(shape) for shape in sems for _ in range(2)],
         compiler_params=pltpu.CompilerParams(collective_id=1, has_side_effects=True),
-    )(part, param, coef, neighbours)
+    )(part, param, kappa, coupling, neighbours)
 
 
 LAST = (((1,), (1,)), ((), ()))
@@ -498,8 +506,7 @@
     part = back_project(
         kernel, weighted, turned, sensors, size, padded, blocks
     )
-    coef = jnp.stack([coupling, kappa_field + 4.0 * coupling], 0)
-    gradient, direction = field_stage(part, flat, coef, neighbours)
+    gradient, direction = field_stage(part, flat, kappa_field[None], coupling[None], neighbours.T)
     return gradient.reshape(param.shape), direction.reshape(param.shape)
 
 

time: 83.5 us -> 78.9 us (0.945)
  local copies, waits for them, and re-layouts: 11.2 us -> 8.54 us
  other arithmetic: 2 us -> 0 us
    unnamed x1 -> x0, local copies, waits for them, and re-layouts: 1.35 us -> none
    broadcast_in_dim x1 -> x0, local copies, waits for them, and re-layouts: 1.32 us -> none  [residual(): spread = jnp.broadcast_to(noise_scale[:, None], observed.shape)]
    another operation x1 -> x0, other arithmetic: 1.29 us -> none  [per_device(): coef = jnp.stack([coupling, kappa_field + 4.0 * coupling], 0)]
where the time goes in v5:
time: 78.9 us; the launch traced here: 78.6 us
  Pallas kernels  69.4 us (88%)
  local copies, waits for them, and re-layouts  8.54 us (11%)
    pallas_call x1, Pallas kernels, field_stage(): pl.pallas_call(functools.partial(field_kernel, groups, tiles), out_shape=...  41 us
    pallas_call x1, Pallas kernels, residual(): pl.pallas_call(functools.partial(residual_kernel, tiles), out_shape=jax.S...  9.87 us
    pallas_call x1, Pallas kernels, predict(): pl.pallas_call(functools.partial(predict_kernel, padded), out_shape=jax.S...  9.85 us
    pallas_call x1, Pallas kernels, back_project(): pl.pallas_call(functools.partial(backward_kernel, padded, blocks), out_sh...  8.75 us
    reshape x2, local copies, waits for them, and re-layouts, per_device(): return (gradient.reshape(param.shape), direction.reshape(param.shape))  5.62 us
    reshape x1, local copies, waits for them, and re-layouts, per_device(): flat = param.reshape(blocks)  2.91 us

profile of v5, /device:TPU:0, one launch (start us, length us, event | category | flops | bytes accessed | tf_op | source)
XLA Modules:
  0.0 78.6 jit_solution(7174137509404984895)
XLA Ops:
  0.6 2.9 %reshape.13.param = f32[32,8,1024]{2,1,0:T(8,128)} reshape(f32[128,2,1024]{2,1,0:T(2,128)} %param.12) | data formatting | bytes 2097152 | tf_op jit(solution)/shard_map/reshape | solution.py:498
  3.5 9.9 %shard_map.122.series = f32[16,256]{1,0:T(8,128)} custom-call(bf16[2,129,16,1024]{3,2,1,0:T(8,128)(2,1)} %kernel.3, f32[32,8,1024]{2,1,0:T(8,128)} %reshape.13.param, bf16[3,2,176,256]{3,2,1,0:T(8,128)(2,1)} %constant.6.clone.fields, bf16[3,2,2,176,256]{4,3,2,1,0:T(8,128)(2,1)} %constant.7.clone.sensors), custom_call_target="tpu_custom_call" | custom-call | tf_op jit(solution)/shard_map/pallas_call | solution.py:427
  13.4 9.9 %shard_map.123.weighted = f32[16,256]{1,0:T(8,128)} custom-call(f32[16,256]{1,0:T(8,128)} %shard_map.122.series, f32[16,128]{1,0:T(8,128)} %observed.1, f32[1,16]{1,0:T(1,128)} %bitcast.7, s32[16,128]{1,0:T(8,128)} %flags.1), custom_call_target="tpu_custom_call" | custom-call | tf_op jit(solution)/shard_map/pallas_call | solution.py:83
  23.3 8.7 %shard_map.124.part = bf16[32,8,1024]{2,1,0:T(8,128)(2,1)} custom-call(bf16[2,129,16,1024]{3,2,1,0:T(8,128)(2,1)} %kernel.3, f32[16,256]{1,0:T(8,128)} %shard_map.123.weighted, bf16[3,2,256,176]{3,2,1,0:T(8,128)(2,1)} %constant.8.clone.fields, bf16[3,2,2,176,256]{4,3,2,1,0:T(8,128)(2,1)} %constant.7.clone.sensors), custom_call_target="tpu_custom_call" | custom-call | tf_op jit(solution)/shard_map/pallas_call | solution.py:476
  32.0 41.0 %shard_map.125 = (f32[32,8,1024]{2,1,0:T(8,128)}, f32[32,8,1024]{2,1,0:T(8,128)}) custom-call(bf16[32,8,1024]{2,1,0:T(8,128)(2,1)} %shard_map.124.part, f32[32,8,1024]{2,1,0:T(8,128)} %reshape.13.param, f32[1,1024]{1,0:T(1,128)} %bitcast.4, f32[1,1024]{1,0:T(1,128)} %bitcast.5, s32[4,8]{1,0:T(4,128)} %bitcast.6), custom_call_target="tpu_custom_call" | custom-call | tf_op jit(solution)/shard_map/pallas_call | solution.py:318
  73.0 2.8 %reshape.14 = f32[128,2,1024]{2,1,0:T(2,128)} reshape(f32[32,8,1024]{2,1,0:T(8,128)} %get-tuple-element.4) | data formatting | bytes 2097152 | tf_op jit(solution)/shard_map/reshape | solution.py:510
  75.8 2.8 %reshape.15 = f32[128,2,1024]{2,1,0:T(2,128)} reshape(f32[32,8,1024]{2,1,0:T(8,128)} %get-tuple-element.5) | data formatting | bytes 2097152 | tf_op jit(solution)/shard_map/reshape | solution.py:510
